TPU v7x, 256 devices: a whole 4x4x8 slice. The times are simulated.
256 devices in a mesh: seq: 16 (over z, x_hi), head: 16 (over x_lo, y, core).
Axes of the slice: x: 4 (x_hi: 2, x_lo: 2; x = x_hi * 2 + x_lo), y: 4, z: 8, core: 2. Of those that a mesh axis runs over, the one named last changes fastest.
Arguments:
- embedded: bfloat16 [2048, 8192], P('seq'), may hold values from -1457.645 to 1457.645
- norm_gain: bfloat16 [8192], replicated, may hold values from 0.5 to 1.5
- query_weight: bfloat16 [8192, 4096], P(None, 'head'), may hold values from -0.125 to 0.125
- query_bias: bfloat16 [4096], P('head'), may hold values from -15 to 15
- key_weight: bfloat16 [8192, 4, 128], P(None, None, 'head'), may hold values from -0.16572815 to 0.16572815
- value_weight: bfloat16 [8192, 4, 128], P(None, None, 'head'), may hold values from -0.0625 to 0.0625
- value_bias: bfloat16 [4, 128], P(None, 'head'), may hold values from -3 to 3
- image_rows: bfloat16 [768, 8192], P('seq'), may hold values from -6 to 6
- image_dest: int32 [768], P('seq'), may hold values from 0 to 2047, as said below
- doc_lengths: int32 [32], replicated, may hold values from 1 to 1152, 2048 in all
- block_mask: int32 [16, 16], P('seq'), may hold values from 0 to 1, as said below
Outputs:
- attention: bfloat16 [2048, 4096], P('seq', 'head')
Inputs may be any that keep to these rules, and one draw needn't show every extreme that they name: `image_dest`: all positions differ. The 48 rows of one owner place at most 6 rows in any one shard of 128 positions, exactly 6 in some shard; one shard takes exactly 6 rows from every owner. `doc_lengths`: they add up to 2048; the longest is exactly 1152. `block_mask`: 1 on the diagonal, 0 above it.
All inputs are finite; a program needn't handle non-finite values.
Results may differ from a plain program's by a relative error of at most 0.011.
Values may be sent and summed in bfloat16 or wider, within the bound.
No kernel may reach another device: no remote copies, remote signals or barrier semaphores. Data moves between devices by JAX's collectives and lax.ppermute only.
A program may use at most 64 MiB of HBM per device.

v0:
```python
import math

import jax
import jax.numpy as jnp
from jax import lax
from jax.sharding import PartitionSpec as P

HD = 128
GROUP = 8
BLK = 128


rope_base = 1000000.0
norm_eps = 1e-06


def rope_tables(position, head_width):
    half_width = head_width // 2
    step_index = jnp.arange(half_width).astype(jnp.float32)
    inverse = jnp.power(jnp.float32(rope_base), -2.0 * step_index / head_width)
    angles = position.astype(jnp.float32)[:, None] * inverse[None, :]
    return (jnp.cos(angles), jnp.sin(angles))


def rotate(vectors, cosine_table, sine_table):
    half_width = vectors.shape[-1] // 2
    leading = vectors[..., :half_width]
    trailing = vectors[..., half_width:]
    cosine_part = cosine_table[:, None, :]
    sine_part = sine_table[:, None, :]
    return jnp.concatenate(
        [
            leading * cosine_part - trailing * sine_part,
            trailing * cosine_part + leading * sine_part,
        ],
        axis=-1,
    )


def doc_numbers(token_index, doc_lengths):
    ends_at = jnp.cumsum(doc_lengths)
    return jnp.sum((token_index[:, None] >= ends_at[None, :]).astype(jnp.int32), axis=1)


def doc_positions(token_index, doc_lengths):
    ends_at = jnp.cumsum(doc_lengths)
    starts = ends_at - doc_lengths
    doc_id = jnp.sum((token_index[:, None] >= ends_at[None, :]).astype(jnp.int32), axis=1)
    start_of = jnp.max(
        jnp.where(token_index[:, None] >= starts[None, :], starts[None, :], 0), axis=1
    )
    return (doc_id, token_index - start_of)


def body(
    embedded,
    norm_gain,
    query_weight,
    query_bias,
    key_weight,
    value_weight,
    value_bias,
    image_rows,
    image_dest,
    doc_lengths,
    block_mask,
):
    tok_rows, model_width = embedded.shape
    seq_place = lax.axis_index("seq")
    head_place = lax.axis_index("head")
    first_row = seq_place * tok_rows
    every_row, every_dest = (
        lax.all_gather(image_rows, "seq", axis=0, tiled=True),
        lax.all_gather(image_dest, "seq", axis=0, tiled=True),
    )
    offset = every_dest - first_row
    inside = (offset >= 0) & (offset < tok_rows)
    merged = embedded.at[jnp.where(inside, offset, tok_rows)].set(every_row, mode="drop")
    widened = merged.astype(jnp.float32)
    inverse_rms = lax.rsqrt(jnp.mean(widened * widened, axis=1, keepdims=True) + norm_eps)
    normed = (widened * inverse_rms * norm_gain.astype(jnp.float32)[None, :]).astype(jnp.bfloat16)
    token_index = first_row + jnp.arange(tok_rows, dtype=jnp.int32)
    doc_id, position = doc_positions(token_index, doc_lengths)
    cosine_table, sine_table = rope_tables(position, HD)
    heads_here = query_weight.shape[1] // HD
    kv_heads = key_weight.shape[1]
    queries = (
        jnp.dot(normed, query_weight, preferred_element_type=jnp.float32)
        + query_bias.astype(jnp.float32)[None, :]
    )
    queries = rotate(queries.reshape(tok_rows, heads_here, HD), cosine_table, sine_table).astype(
        jnp.bfloat16
    )
    key_cols = jnp.dot(
        normed, key_weight.reshape(model_width, -1), preferred_element_type=jnp.float32
    )
    key_cols = key_cols.astype(jnp.bfloat16).reshape(tok_rows, kv_heads, -1)
    value_cols = jnp.dot(
        normed, value_weight.reshape(model_width, -1), preferred_element_type=jnp.float32
    )
    value_cols = (
        (value_cols + value_bias.reshape(-1).astype(jnp.float32)[None, :])
        .astype(jnp.bfloat16)
        .reshape(tok_rows, kv_heads, -1)
    )
    key_full, value_full = (
        lax.all_gather(key_cols, "head", axis=2, tiled=True),
        lax.all_gather(value_cols, "head", axis=2, tiled=True),
    )
    group_place = head_place * heads_here // GROUP
    own_key = lax.dynamic_index_in_dim(key_full, group_place, 1, keepdims=False)
    own_value = lax.dynamic_index_in_dim(value_full, group_place, 1, keepdims=False)
    own_key = rotate(own_key.astype(jnp.float32)[:, None, :], cosine_table, sine_table)[
        :, 0, :
    ].astype(jnp.bfloat16)
    panel = jnp.stack([own_key, own_value])
    scale_factor = 1.0 / math.sqrt(HD)
    mask_rows = jnp.repeat(block_mask, BLK, axis=0).astype(jnp.bfloat16)
    block_total = block_mask.shape[1]
    panel_part = lax.all_gather(panel, "seq", axis=1, tiled=True)
    piece_key = panel_part[0]
    piece_value = panel_part[1]
    key_index = jnp.arange(panel_part.shape[1], dtype=jnp.int32)
    key_docs = doc_numbers(key_index, doc_lengths)
    key_hot = (key_index[:, None] // BLK == jnp.arange(block_total)[None, :]).astype(jnp.bfloat16)
    pair_open = (
        jnp.einsum("tb,sb->ts", mask_rows, key_hot, preferred_element_type=jnp.float32) > 0.5
    )
    allowed = (
        pair_open
        & (key_index[None, :] <= token_index[:, None])
        & (key_docs[None, :] == doc_id[:, None])
        & (key_index[None, :] >= 0)
    )
    prior_max = jnp.full((heads_here, tok_rows), -1e30, jnp.float32)
    scores = (
        jnp.einsum("thd,sd->hts", queries, piece_key, preferred_element_type=jnp.float32)
        * scale_factor
    )
    masked = jnp.where(allowed[None], scores, -jnp.inf)
    fresh_max = jnp.maximum(prior_max, jnp.max(masked, axis=2))
    weights = jnp.where(allowed[None], jnp.exp(scores - fresh_max[:, :, None]), 0.0)
    fresh_total = jnp.sum(weights, axis=2)
    added = jnp.einsum(
        "hts,sd->thd", weights.astype(jnp.bfloat16), piece_value, preferred_element_type=jnp.float32
    )
    final_state = (fresh_max, fresh_total, added)
    final_max, final_total, final_mix = final_state
    attention = final_mix / jnp.transpose(final_total)[:, :, None]
    return attention.reshape(tok_rows, heads_here * HD).astype(jnp.bfloat16)


def solution(mesh):
    in_specs = (
        P("seq", None),
        P(),
        P(None, "head"),
        P("head"),
        P(None, None, "head"),
        P(None, None, "head"),
        P(None, "head"),
        P("seq", None),
        P("seq"),
        P(),
        P("seq", None),
    )
    out_specs = P("seq", "head")
    return jax.shard_map(body, mesh=mesh, in_specs=in_specs, out_specs=out_specs, check_vma=False)
```

profile of v0, /device:TPU:1, one launch (start us, length us, event | category | flops | bytes accessed | tf_op | source)
XLA Modules:
  0.0 335.5 jit_solution(15263415627890601210)
XLA Ops:
  6.6 0.7 all-gather.3.cloned.1.call-update
  7.5 0.1 reduce
  7.8 0.6 dynamic-slice
  9.0 0.2 dynamic-update-slice
  9.3 17.3 %all-reduce = s32[768]{0:T(1024)S(1)} all-reduce(s32[768]{0:T(1024)S(1)} %dynamic-update-slice), channel_id=1, replica_groups=mesh['seq'=16,'head'=16] {'seq'}, use_global_device_ids=true, to_apply=%add | all-reduce | flops 768 | bytes 6144
  26.7 165.4 %all-gather.3.cloned.1.call-done = bf16[768,8192]{1,0:T(8,128)(2,1)} async-done(((bf16[48,8192]{1,0:T(8,128)(2,1)}), bf16[768,8192]{1,0:T(8,128)(2,1)}) %all-gather.3.cloned.1.call-update) | async-done | bytes 12582928 | tf_op jit(solution)/shard_map/all_gather | solution.py:73
  192.1 25.0 %scatter_fusion = bf16[128,8192]{1,0:T(8,128)(2,1)S(1)} fusion(bf16[128,8192]{1,0:T(8,128)(2,1)S(1)} %copy-done.1, s32[768]{0:T(1024)S(1)} %compare_select_fusion, bf16[768,8192]{1,0:T(8,128)(2,1)} %all-gather.3.cloned.1.call-done), kind=kCustom, calls=%fused_computation | custom fusion | bytes 37751808 | tf_op jit(solution)/shard_map/scatter | solution.py:78
  217.1 0.5 fusion
  217.6 0.9 fusion.12
  218.6 19.9 %all_gather.17 = bf16[128,4,128]{0,1,2:T(4,128)(2,1)S(1)} all-gather(bf16[128,4,8]{0,1,2:T(4,128)(2,1)S(1)} %copy.46), channel_id=1, replica_groups=mesh['seq'=16,'head'=16] {'head'}, dimensions={2}, use_global_device_ids=true | all-gather | bytes 139264 | tf_op jit(solution)/shard_map/all_gather | solution.py:107
  238.6 0.9 fusion.13
  239.5 16.6 %all_gather.18 = bf16[128,4,128]{0,2,1:T(8,128)(2,1)S(1)} all-gather(bf16[128,4,8]{0,2,1:T(8,128)(2,1)S(1)} %fusion.13), channel_id=1, replica_groups=mesh['seq'=16,'head'=16] {'head'}, dimensions={2}, use_global_device_ids=true | all-gather | bytes 139264 | tf_op jit(solution)/shard_map/all_gather | solution.py:108
  256.1 0.2 fusion.29
  256.3 0.6 pad_maximum_fusion
  257.0 0.1 convert_reduce_fusion
  257.2 0.3 multiply_cosine_fusion
  257.5 1.9 fusion.6
  259.4 2.9 convolution_add_fusion
  262.4 0.2 fusion.41
  262.6 62.6 %all-gather.5.cloned.1.call-done = bf16[2,2048,128]{1,2,0:T(8,128)(2,1)} async-done(((bf16[2,128,128]{1,2,0:T(8,128)(2,1)}), bf16[2,2048,128]{1,2,0:T(8,128)(2,1)}) %all-gather.5.cloned.1.call-update) | async-done | bytes 1048592 | tf_op jit(solution)/shard_map/all_gather | solution.py:120
  325.2 1.7 select_reduce_fusion
  327.0 0.4 fusion.7
  327.4 0.5 fusion.10
  327.9 0.7 copy.53
  (48 shorter events, 0.7 us)
Async XLA Ops:
  6.5 211.1 %copy-start = (bf16[8192,4,8]{0,2,1:T(8,128)(2,1)S(1)}, bf16[8192,4,8]{0,2,1:T(8,128)(2,1)}, u32[]{:S(2)}) copy-start(bf16[8192,4,8]{0,2,1:T(8,128)(2,1)} %param.15) | copy-start | bytes 1572868
  6.5 0.8 copy-start.2
  6.5 1.1 copy-start.6
  6.5 1.2 copy-start.10
  6.5 185.5 %copy-start.1 = (bf16[128,8192]{1,0:T(8,128)(2,1)S(1)}, bf16[128,8192]{1,0:T(8,128)(2,1)}, u32[]{:S(2)}) copy-start(bf16[128,8192]{1,0:T(8,128)(2,1)} %param.11) | copy-start | bytes 6291460
  6.5 2.5 copy-start.7
  6.6 0.8 copy-start.3
  6.6 185.5 %all-gather.3.cloned.1.call-start = ((), (), s32[]{:S(2)}) async-start(), calls=%async_computation | async-start | bytes 13369344 | tf_op jit(solution)/shard_map/all_gather | solution.py:73
  7.3 317.9 %all-gather.5.cloned.1.call-start = ((), (), s32[]{:S(2)}) async-start(), calls=%async_computation.1 | async-start | bytes 1114112 | tf_op jit(solution)/shard_map/all_gather | solution.py:120
  217.6 21.0 %copy-start.5 = (bf16[8192,4,8]{0,2,1:T(8,128)(2,1)S(1)}, bf16[8192,4,8]{0,2,1:T(8,128)(2,1)}, u32[]{:S(2)}) copy-start(bf16[8192,4,8]{0,2,1:T(8,128)(2,1)} %param.16) | copy-start | bytes 1572868
  238.6 18.4 %copy-start.8 = (bf16[256]{0:T(256)(128)(2,1)S(1)}, bf16[256]{0:T(256)(128)(2,1)}, u32[]{:S(2)}) copy-start(bf16[256]{0:T(256)(128)(2,1)} %param.14) | copy-start | bytes 1540
  238.6 18.6 %copy-start.9 = (s32[1,16]{1,0:T(1,128)S(1)}, s32[1,16]{1,0:T(1,128)}, u32[]{:S(2)}) copy-start(s32[1,16]{1,0:T(1,128)} %param.21) | copy-start | bytes 196
  325.2 2.2 copy-start.4
Sparse Core Ops, SparseCore 0:
  10.0 182.0 all-gather.2
  257.1 68.0 all-gather.4
where the time goes:
time: 338 us; the launch traced here: 336 us
  waiting for transfers between devices  229 us (68%)
  blocking collectives  53.8 us (16%)
  local copies, waits for them, and re-layouts  27.2 us (8%)
  between operations  14.4 us (4%)
  matrix products  8.84 us (3%)
    all_gather x1, waiting for transfers between devices, body(): lax.all_gather(image_rows, 'seq', axis=0, tiled=True)  165 us
    all_gather x1, waiting for transfers between devices, body(): panel_part = lax.all_gather(panel, 'seq', axis=1, tiled=True)  62.6 us
    scatter x1, local copies, waits for them, and re-layouts, body(): embedded.at[jnp.where(inside, offset, tok_rows)].set(every_row, mode='drop')  25 us
    all_gather x1, blocking collectives, body(): lax.all_gather(key_cols, 'head', axis=2, tiled=True)  19.9 us
    unnamed x1, blocking collectives  17.3 us
    all_gather x1, blocking collectives, body(): lax.all_gather(value_cols, 'head', axis=2, tiled=True)  16.6 us
  transfers between devices with their start and end apart: 2, of which 2 were waited for; matrix products, arithmetic and copies ran while one was open for 2% of the time, Pallas kernels for 0%

commit v1 on v0

v1 whole, which is shorter than its diff:
```python
import functools
import math

import jax
import jax.numpy as jnp
import numpy as np
from jax import lax
from jax.experimental import pallas as pl
from jax.experimental.pallas import tpu as pltpu
from jax.sharding import PartitionSpec as P

HD = 128
GROUP = 8
BLK = 128
CAP = 6
TOK = 128
IMG = 48
ROWS = TOK + IMG
TAIL = 16
PAY = ROWS + TAIL
N_SEQ = 16
N_HEAD = 16
DOCS = 32
KCH = 4
LIMIT = 60 << 20
SMALL = 12 << 20

rope_base = 1000000.0
norm_eps = 1e-06
BIG = 1.0e6
NEG = -1.0e30

f32 = jnp.float32
bf16 = jnp.bfloat16


def iota(shape, dim):
    return lax.broadcasted_iota(jnp.int32, shape, dim)


def fiota(shape, dim):
    return iota(shape, dim).astype(f32)


def dot_t(a, b):
    return lax.dot_general(a, b, (((1,), (1,)), ((), ())), preferred_element_type=f32)


def tdot(a, b):
    return lax.dot_general(a, b, (((0,), (0,)), ((), ())), preferred_element_type=f32)


def project_kernel(
    x_hbm, img_hbm, wq_hbm, wk_hbm, wv_hbm, gain_hbm, bq_hbm, bv_hbm, dest_hbm, invf_hbm, docs_ref,
    q_ref, kv_ref, tail_hbm, cs_hbm, start_hbm,
    xs, wqs, wkvs, gains, bqs, bvs, dests, invfs, tails, css, starts, sems, small_sems, out_sems,
):
    width = xs.shape[1]
    step = width // KCH
    copies = [
        pltpu.make_async_copy(x_hbm, xs.at[pl.ds(0, TOK)], sems.at[0]),
        pltpu.make_async_copy(img_hbm, xs.at[pl.ds(TOK, IMG)], sems.at[1]),
        pltpu.make_async_copy(wk_hbm, wkvs.at[pl.ds(0, 32)], sems.at[2]),
        pltpu.make_async_copy(wv_hbm, wkvs.at[pl.ds(32, 32)], sems.at[3]),
    ]
    for c in range(KCH):
        part = pl.ds(c * step, step)
        copies.append(pltpu.make_async_copy(wq_hbm.at[part], wqs.at[part], sems.at[4 + c]))
    small = [
        pltpu.make_async_copy(src, dst, small_sems.at[i])
        for i, (src, dst) in enumerate(
            ((dest_hbm, dests), (invf_hbm, invfs), (gain_hbm, gains), (bq_hbm, bqs), (bv_hbm, bvs))
        )
    ]
    for copy in small[:2] + copies[:2] + small[2:] + copies[2:]:
        copy.start()
    small[0].wait()
    small[1].wait()

    seq_place = lax.axis_index("seq")
    first = (seq_place * TOK).astype(f32)
    dest_row = dests[...].astype(f32)
    eye = iota((IMG, IMG), 0) == iota((IMG, IMG), 1)
    dest_col = jnp.sum(jnp.where(eye, dest_row, 0.0), axis=1, keepdims=True)
    hi_row = jnp.floor(dest_row * (1.0 / TOK))
    hi_col = jnp.floor(dest_col * (1.0 / TOK))
    lo_row = dest_row - TOK * hi_row
    lo_col = dest_col - TOK * hi_col

    index_col = jnp.concatenate([first + fiota((TOK, 1), 0), dest_col], axis=0)
    start_col = jnp.zeros((ROWS, 1), f32)
    begin = jnp.int32(0)
    for d in range(DOCS):
        begin_f = begin.astype(f32)
        start_col = jnp.where(index_col >= begin_f, begin_f, start_col)
        begin = begin + docs_ref[d]
    starts[...] = jnp.broadcast_to(start_col[:TOK], (TOK, HD))
    angles = (index_col - start_col) * invfs[...]
    cosine = jnp.cos(angles)
    sine = jnp.sin(angles)
    css[0] = cosine
    css[1] = jnp.where(iota((ROWS, HD), 1) < HD // 2, -sine, sine)

    earlier = iota((IMG, IMG), 0) < iota((IMG, IMG), 1)
    later = iota((IMG, IMG), 0) > iota((IMG, IMG), 1)
    same = hi_col == hi_row
    rank_row = jnp.sum(jnp.where(same & earlier, 1.0, 0.0), axis=0, keepdims=True)
    rank_col = jnp.sum(jnp.where(same & later, 1.0, 0.0), axis=1, keepdims=True)
    count = N_SEQ * TAIL
    line = iota((count, IMG), 0)
    here = hi_row == (line // TAIL).astype(f32)
    slot = (line % TAIL).astype(f32)
    offsets = jnp.where(here & (slot == 14.0), lo_row + 1.0, 0.0).astype(bf16)
    lane = iota((IMG, HD), 1)
    ranked = jnp.where((rank_col == lane.astype(f32)) & (lane < CAP), 1.0, 0.0).astype(bf16)
    tail = jnp.dot(offsets, ranked, preferred_element_type=f32)
    spread = (lane % 64) == iota((IMG, HD), 0)
    unused = (iota((1, HD), 1) % 64) >= IMG
    hi_two = jnp.where(unused, 99.0, jnp.sum(jnp.where(spread, hi_col, 0.0), axis=0, keepdims=True))
    lo_two = jnp.sum(jnp.where(spread, lo_col, 0.0), axis=0, keepdims=True)
    wide_slot = iota((count, HD), 0) % TAIL
    tail = tail + jnp.where(wide_slot == 12, hi_two, jnp.where(wide_slot == 13, lo_two, 0.0))

    outs = [
        pltpu.make_async_copy(css, cs_hbm, out_sems.at[0]),
        pltpu.make_async_copy(starts, start_hbm, out_sems.at[1]),
        pltpu.make_async_copy(tails, tail_hbm, out_sems.at[2]),
    ]
    outs[0].start()
    outs[1].start()

    inverse = []
    for i, rows in enumerate((pl.ds(0, TOK), pl.ds(TOK, IMG))):
        copies[i].wait()
        squares = jnp.zeros((rows.size, HD), f32)
        for c in range(width // HD):
            wide = xs[rows, c * HD : (c + 1) * HD].astype(f32)
            squares = squares + wide * wide
        inverse.append(
            lax.rsqrt(jnp.sum(squares, axis=1, keepdims=True) * (1.0 / width) + norm_eps)
        )
    inverse = jnp.concatenate(inverse, axis=0)

    for copy in small[2:] + copies[2:4]:
        copy.wait()
    queries = jnp.broadcast_to(bqs[...].astype(f32).reshape(1, 2 * HD), (ROWS, 2 * HD))
    kv = jnp.zeros((ROWS, 64), f32)
    for c in range(KCH):
        copies[4 + c].wait()
        part = pl.ds(c * step, step)
        gain = gains[part].astype(f32).reshape(1, step)
        normed = (xs[:, part].astype(f32) * inverse * gain).astype(bf16)
        kv = kv + dot_t(normed, wkvs[:, part])
        queries = queries + jnp.dot(normed, wqs[part, :], preferred_element_type=f32)

    kv = jnp.concatenate([kv, jnp.zeros((ROWS, 64), f32)], axis=1)
    kv = jnp.concatenate([kv, jnp.zeros((256 - ROWS, 128), f32)], axis=0)
    kv_t = jnp.transpose(kv)
    eye8 = iota((8, 8), 0) == iota((8, 8), 1)
    for g in range(4):
        key = kv_t[8 * g : 8 * g + 8].astype(bf16)
        bias_row = bvs[g : g + 1, :].astype(f32)
        bias = jnp.sum(jnp.where(eye8, bias_row, 0.0), axis=1, keepdims=True)
        value = (kv_t[32 + 8 * g : 40 + 8 * g] + bias).astype(bf16)
        for j in range(2):
            kv_ref[4 * g + 2 * j] = key
            kv_ref[4 * g + 2 * j + 1] = value

    cosine = css[0]
    sine = css[1]
    for e in range(2):
        v = queries[:, e * HD : (e + 1) * HD]
        v = (v * cosine + pltpu.roll(v, HD // 2, 1) * sine).astype(bf16)
        q_ref[e] = v[:TOK]
        pick = here & (rank_row == slot - CAP * e) & (slot >= CAP * e) & (slot < CAP * e + CAP)
        tail = tail + jnp.dot(
            jnp.where(pick, 1.0, 0.0).astype(bf16), v[TOK:], preferred_element_type=f32
        )
    tails[...] = tail.astype(bf16).reshape(N_SEQ, TAIL, HD)
    outs[2].start()
    for out in outs:
        out.wait()


def panel_kernel(kv_ref, cs_ref, tail_ref, pay_ref):
    is_key = lax.axis_index("head") % 2 == 0
    panel = jnp.transpose(kv_ref[...].astype(f32).reshape(HD, 256))[:ROWS]
    cosine = jnp.where(is_key, cs_ref[0], 1.0)
    sine = jnp.where(is_key, cs_ref[1], 0.0)
    panel = (panel * cosine + pltpu.roll(panel, HD // 2, 1) * sine).astype(bf16)
    for p in range(N_SEQ):
        pay_ref[p, 0:ROWS, :] = panel
        pay_ref[p, ROWS:PAY, :] = tail_ref[p]


def place_kernel(q_ref, mine_ref, mask_ref, merged_ref, where_ref):
    tails = mine_ref[:, ROWS:PAY, :].astype(f32)
    hi_all = tails[:, 12, :]
    lo_all = tails[:, 13, :]
    slots = tails[:, 14, :]
    count = N_SEQ * TAIL
    owner = iota((count, N_SEQ), 0) // TAIL == iota((count, N_SEQ), 1)
    spread = jnp.dot(
        jnp.where(owner, 1.0, 0.0).astype(bf16), slots.astype(bf16), preferred_element_type=f32
    )
    line = iota((count, HD), 0) % TAIL
    lane = iota((count, HD), 1)
    flat = mine_ref[:, ROWS:PAY, :].reshape(count, HD)
    for e in range(2):
        slot = line - CAP * e
        used = (slot >= 0) & (slot < CAP)
        offset = jnp.sum(jnp.where(used & (lane == slot), spread, 0.0), axis=1, keepdims=True)
        place = jnp.where(offset == lane.astype(f32) + 1.0, 1.0, 0.0).astype(bf16)
        moved = tdot(place, flat)
        taken = tdot(place, jnp.ones((count, HD), bf16))
        merged_ref[e * TOK : (e + 1) * TOK, :] = jnp.where(taken > 0.5, moved.astype(bf16), q_ref[e])

    low_half = iota((1, HD), 1) < 64
    covered = jnp.zeros((N_SEQ, HD), f32)
    for m in range(N_SEQ // 2):
        hi = jnp.where(low_half, hi_all[2 * m : 2 * m + 1], hi_all[2 * m + 1 : 2 * m + 2])
        lo = jnp.where(low_half, lo_all[2 * m : 2 * m + 1], lo_all[2 * m + 1 : 2 * m + 2])
        hi_hot = jnp.where(hi == fiota((N_SEQ, HD), 0), 1.0, 0.0).astype(bf16)
        lo_hot = jnp.where(lo == fiota((HD, HD), 0), 1.0, 0.0).astype(bf16)
        covered = covered + dot_t(hi_hot, lo_hot)
        seen = jnp.zeros((1, HD), f32)
        for b in range(N_SEQ):
            seen = jnp.where(hi == float(b), mask_ref[0, b].astype(f32), seen)
        where_ref[N_SEQ + m : N_SEQ + m + 1, :] = jnp.where(seen > 0.5, hi * float(TOK) + lo, BIG)
    for b in range(N_SEQ):
        free = (covered[b : b + 1] < 0.5) & (mask_ref[0, b] == 1)
        where_ref[b : b + 1, :] = jnp.where(free, float(TOK * b) + fiota((1, HD), 1), BIG)


def attend_kernel(q_ref, where_ref, start_ref, mine_ref, other_ref, out_ref, scores):
    is_key = lax.axis_index("head") % 2 == 0
    first = (lax.axis_index("seq") * TOK).astype(f32)
    tiles = N_SEQ + N_SEQ // 2
    slope = math.log2(math.e) / math.sqrt(HD)

    def tile_of(ref, t):
        if t < N_SEQ:
            return ref[t, 0:TOK, :]
        m = t - N_SEQ
        return ref[2 * m : 2 * m + 2, TOK:PAY, :].reshape(HD, HD)

    def attend(keys, values):
        queries = q_ref[...]
        position = first + fiota((TOK, HD), 0)
        start = start_ref[...]
        top = jnp.full((2 * TOK, HD), NEG, f32)
        for t in range(tiles):
            where = where_ref[t : t + 1, :]
            allowed = (where <= position) & (where >= start)
            allowed = jnp.concatenate([allowed, allowed], axis=0)
            score = jnp.where(allowed, dot_t(queries, tile_of(keys, t)), NEG)
            scores[t] = score
            top = jnp.maximum(top, score)
        top = jnp.max(top, axis=1, keepdims=True)
        total = jnp.zeros((2 * TOK, HD), f32)
        mix = jnp.zeros((2 * TOK, HD), f32)
        for t in range(tiles):
            weight = jnp.exp2((scores[t] - top) * slope)
            total = total + weight
            mix = mix + jnp.dot(weight.astype(bf16), tile_of(values, t), preferred_element_type=f32)
        mix = mix / jnp.sum(total, axis=1, keepdims=True)
        out_ref[:, 0:HD] = mix[:TOK].astype(bf16)
        out_ref[:, HD : 2 * HD] = mix[TOK:].astype(bf16)

    @pl.when(is_key)
    def _():
        attend(mine_ref, other_ref)

    @pl.when(jnp.logical_not(is_key))
    def _():
        attend(other_ref, mine_ref)


def vmem():
    return pl.BlockSpec(memory_space=pltpu.VMEM)


def body(
    embedded,
    norm_gain,
    query_weight,
    query_bias,
    key_weight,
    value_weight,
    value_bias,
    image_rows,
    image_dest,
    doc_lengths,
    block_mask,
):
    width = embedded.shape[1]
    half = np.arange(HD) % (HD // 2)
    inverse = jnp.asarray((rope_base ** (-2.0 * half / HD)).astype(np.float32)[None, :])
    hbm = pl.BlockSpec(memory_space=pltpu.HBM)
    smem = pl.BlockSpec(memory_space=pltpu.SMEM)
    key_t = jnp.transpose(key_weight, (1, 2, 0)).reshape(32, width)
    value_t = jnp.transpose(value_weight, (1, 2, 0)).reshape(32, width)
    queries, kv_send, tail, tables, start = pl.pallas_call(
        project_kernel,
        name="project",
        out_shape=(
            jax.ShapeDtypeStruct((2, TOK, HD), bf16),
            jax.ShapeDtypeStruct((N_HEAD, 8, 256), bf16),
            jax.ShapeDtypeStruct((N_SEQ, TAIL, HD), bf16),
            jax.ShapeDtypeStruct((2, ROWS, HD), f32),
            jax.ShapeDtypeStruct((TOK, HD), f32),
        ),
        in_specs=[hbm] * 10 + [smem],
        out_specs=(vmem(), vmem(), hbm, hbm, hbm),
        scratch_shapes=[
            pltpu.VMEM((ROWS, width), bf16),
            pltpu.VMEM((width, 2 * HD), bf16),
            pltpu.VMEM((64, width), bf16),
            pltpu.VMEM((width,), bf16),
            pltpu.VMEM((2 * HD,), bf16),
            pltpu.VMEM((4, 8), bf16),
            pltpu.VMEM((1, IMG), jnp.int32),
            pltpu.VMEM((1, HD), f32),
            pltpu.VMEM((N_SEQ, TAIL, HD), bf16),
            pltpu.VMEM((2, ROWS, HD), f32),
            pltpu.VMEM((TOK, HD), f32),
            pltpu.SemaphoreType.DMA((4 + KCH,)),
            pltpu.SemaphoreType.DMA((5,)),
            pltpu.SemaphoreType.DMA((3,)),
        ],
        compiler_params=pltpu.CompilerParams(vmem_limit_bytes=LIMIT),
    )(
        embedded, image_rows, query_weight, key_t, value_t, norm_gain, query_bias,
        value_bias, image_dest[None, :], inverse, doc_lengths,
    )
    kv_mine = lax.all_to_all(kv_send, "head", 0, 0)
    payload = pl.pallas_call(
        panel_kernel,
        name="panel",
        out_shape=jax.ShapeDtypeStruct((N_SEQ, PAY, HD), bf16),
        in_specs=[vmem()] * 3,
        out_specs=vmem(),
        compiler_params=pltpu.CompilerParams(vmem_limit_bytes=LIMIT),
    )(kv_mine, tables, tail)
    mine = lax.all_to_all(payload, "seq", 0, 0)
    other = lax.ppermute(mine, "head", [(i, i ^ 1) for i in range(N_HEAD)])
    merged, where = pl.pallas_call(
        place_kernel,
        name="place",
        out_shape=(
            jax.ShapeDtypeStruct((2 * TOK, HD), bf16),
            jax.ShapeDtypeStruct((N_SEQ + N_SEQ // 2, HD), f32),
        ),
        in_specs=[vmem(), vmem(), smem],
        out_specs=(vmem(), vmem()),
        compiler_params=pltpu.CompilerParams(vmem_limit_bytes=SMALL),
        cost_estimate=pl.CostEstimate(flops=1 << 28, bytes_accessed=1 << 20, transcendentals=0),
    )(queries, mine, block_mask)
    return pl.pallas_call(
        attend_kernel,
        name="attend",
        out_shape=jax.ShapeDtypeStruct((TOK, 2 * HD), bf16),
        in_specs=[vmem()] * 5,
        out_specs=vmem(),
        scratch_shapes=[pltpu.VMEM((N_SEQ + N_SEQ // 2, 2 * TOK, HD), f32)],
        compiler_params=pltpu.CompilerParams(vmem_limit_bytes=SMALL),
    )(merged, where, start, mine, other)


def solution(mesh):
    in_specs = (
        P("seq", None),
        P(),
        P(None, "head"),
        P("head"),
        P(None, None, "head"),
        P(None, None, "head"),
        P(None, "head"),
        P("seq", None),
        P("seq"),
        P(),
        P("seq", None),
    )
    out_specs = P("seq", "head")
    return jax.shard_map(body, mesh=mesh, in_specs=in_specs, out_specs=out_specs, check_vma=False)
```

time: 338 us -> 65.3 us (0.19)
  waiting for transfers between devices: 229 us -> 0.01 us
  local copies, waits for them, and re-layouts: 27.2 us -> 1.68 us
  between operations: 14.4 us -> 0.03 us
  Pallas kernels: 0 us -> 14.2 us
  matrix products: 8.84 us -> 0 us
  blocking collectives: 53.8 us -> 47 us
    all_gather x2 -> x0, waiting for transfers between devices: 228 us -> none  [the longest x1 165 us: body(): lax.all_gather(image_rows, 'seq', axis=0, tiled=True)]
    all_to_all x0 -> x2, blocking collectives: none -> 47 us  [the longest x1 33.9 us: body(): mine = lax.all_to_all(payload, 'seq', 0, 0)]
    all_gather x2 -> x0, blocking collectives: 36.5 us -> none  [the longest x1 19.9 us: body(): lax.all_gather(key_cols, 'head', axis=2, tiled=True)]
    scatter x1 -> x0, local copies, waits for them, and re-layouts: 25 us -> none  [body(): embedded.at[jnp.where(inside, offset, tok_rows)].set(every_row, mode='drop')]
    unnamed x1 -> x0, blocking collectives: 17.3 us -> none
    pallas_call x0 -> x4, Pallas kernels: none -> 14.2 us  [the longest x1 7.94 us: body(): pl.pallas_call(project_kernel, name='project', out_shape=(jax.ShapeDtypeS...]
    dot_general x6 -> x0, matrix products: 8.84 us -> none  [the longest x1 2.95 us: body(): jnp.dot(normed, query_weight, preferred_element_type=jnp.float32)]
  transfers between devices with their start and end apart: 2 -> 1, of which waited for: 2 -> 0; matrix products, arithmetic and copies ran while one was open for 2% -> 0% of each run, Pallas kernels for 0% -> 2%
where the time goes in v1:
time: 65.3 us; the launch traced here: 65 us
  blocking collectives  47 us (72%)
  Pallas kernels  14.2 us (22%)
  starting transfers between devices  2.05 us (3%)
  local copies, waits for them, and re-layouts  1.68 us (3%)
    all_to_all x1, blocking collectives, body(): mine = lax.all_to_all(payload, 'seq', 0, 0)  33.9 us
    all_to_all x1, blocking collectives, body(): kv_mine = lax.all_to_all(kv_send, 'head', 0, 0)  13.1 us
    pallas_call x1, Pallas kernels, body(): pl.pallas_call(project_kernel, name='project', out_shape=(jax.ShapeDtypeS...  7.94 us
    pallas_call x1, Pallas kernels, body(): pl.pallas_call(attend_kernel, name='attend', out_shape=jax.ShapeDtypeStru...  2.94 us
    pallas_call x1, Pallas kernels, body(): pl.pallas_call(panel_kernel, name='panel', out_shape=jax.ShapeDtypeStruct...  2.07 us
    ppermute x1, starting transfers between devices, body(): other = lax.ppermute(mine, 'head', [(i, i ^ 1) for i in range(N_HEAD)])  2.05 us
    unnamed x6, local copies, waits for them, and re-layouts  1.68 us
  transfers between devices with their start and end apart: 1, of which 0 were waited for; matrix products, arithmetic and copies ran while one was open for 0% of the time, Pallas kernels for 2%

profile of v1, /device:TPU:1, one launch (start us, length us, event | category | flops | bytes accessed | tf_op | source)
XLA Modules:
  0.0 65.0 jit_solution(15588727683258630109)
XLA Ops:
  0.0 0.0 copy-start.2
  0.0 7.9 %project.1 = (bf16[2,128,128]{2,1,0:T(8,128)(2,1)}, bf16[16,8,256]{2,1,0:T(8,128)(2,1)}, bf16[16,16,128]{2,1,0:T(8,128)(2,1)}, f32[2,176,128]{2,1,0:T(8,128)}, f32[128,128]{1,0:T(8,128)}) custom-call(bf16[128,8192]{1,0:T(8,128)(2,1)} %x_hbm.1, bf16[48,8192]{1,0:T(8,128)(2,1)} %img_hbm.1, bf16[8192,256]{1,0:T(8,128)(2,1)} %wq_hbm.1, ...), custom_call_target="tpu_custom_call" | custom-call | tf_op jit(solution)/shard_map/project/pallas_call | solution.py:303
  8.0 13.1 %all_to_all.10.kv_ref = bf16[16,8,256]{2,1,0:T(8,128)(2,1)} all-to-all(bf16[16,8,256]{2,1,0:T(8,128)(2,1)} %get-tuple-element.13), channel_id=1, replica_groups=mesh['seq'=16,'head'=16] {'head'}, dimensions={0} | all-to-all | bytes 131072 | tf_op jit(solution)/shard_map/all_to_all | solution.py:336
  21.1 2.1 %panel.1 = bf16[16,192,128]{2,1,0:T(8,128)(2,1)} custom-call(bf16[16,8,256]{2,1,0:T(8,128)(2,1)} %all_to_all.10.kv_ref, f32[2,176,128]{2,1,0:T(8,128)} %get-tuple-element.14.cs_ref, bf16[16,16,128]{2,1,0:T(8,128)(2,1)} %get-tuple-element.15.tail_ref), custom_call_target="tpu_custom_call" | custom-call | tf_op jit(solution)/shard_map/panel/pallas_call | solution.py:337
  23.1 33.9 %all_to_all.11.mine_ref = bf16[16,192,128]{2,1,0:T(8,128)(2,1)S(1)} all-to-all(bf16[16,192,128]{2,1,0:T(8,128)(2,1)} %panel.1), channel_id=1, replica_groups=mesh['seq'=16,'head'=16] {'seq'}, dimensions={0} | all-to-all | bytes 1572864 | tf_op jit(solution)/shard_map/all_to_all | solution.py:345
  57.1 2.0 %collective-permute-start = (bf16[16,192,128]{2,1,0:T(8,128)(2,1)S(1)}, bf16[16,192,128]{2,1,0:T(8,128)(2,1)S(1)}, u32[]{:S(2)}, u32[]{:S(2)}) collective-permute-start(bf16[16,192,128]{2,1,0:T(8,128)(2,1)S(1)} %all_to_all.11.mine_ref), channel_id=1, source_target_pairs={{0,1},{1,0},{2,3},{3,2},{4,5},{5,4},{6,7},{7,6},{8,9},{9,8},{10,11... | collective-permute-start | bytes 2359304 | tf_op jit(solution)/shard_map/ppermute | solution.py:346
  59.1 0.0 copy-done.2
  59.1 0.0 copy-start.1
  59.1 0.8 %copy-done.1 = bf16[2,128,128]{2,1,0:T(8,128)(2,1)S(1)} copy-done((bf16[2,128,128]{2,1,0:T(8,128)(2,1)S(1)}, bf16[2,128,128]{2,1,0:T(8,128)(2,1)}, u32[]{:S(2)}) %copy-start.1) | copy-done | bytes 65560
  60.0 1.2 %place.1 = (bf16[256,128]{1,0:T(8,128)(2,1)S(1)}, f32[24,128]{1,0:T(8,128)S(1)}) custom-call(bf16[2,128,128]{2,1,0:T(8,128)(2,1)S(1)} %copy-done.1, bf16[16,192,128]{2,1,0:T(8,128)(2,1)S(1)} %all_to_all.11.mine_ref, s32[1,16]{1,0:T(1,128)S(1)} %copy-done.2), custom_call_target="tpu_custom_call" | custom-call | flops 268435456 | bytes 1048576 | tf_op jit(solution)/shard_map/place/pallas_call | solution.py:347
  61.2 0.0 collective-permute-done.other_ref
  61.2 0.0 copy-start
  61.2 0.8 %copy-done = f32[128,128]{1,0:T(8,128)S(1)} copy-done((f32[128,128]{1,0:T(8,128)S(1)}, f32[128,128]{1,0:T(8,128)}, u32[]{:S(2)}) %copy-start) | copy-done | bytes 65560
  62.0 2.9 %attend.1 = bf16[128,256]{1,0:T(8,128)(2,1)} custom-call(bf16[256,128]{1,0:T(8,128)(2,1)S(1)} %get-tuple-element.16.q_ref, f32[24,128]{1,0:T(8,128)S(1)} %get-tuple-element.17.where_ref, f32[128,128]{1,0:T(8,128)S(1)} %copy-done, bf16[16,192,128]{2,1,0:T(8,128)(2,1)S(1)} %all_to_all.11.mine_ref, bf16[16,192,128]{2,1,0:T(8,128)(2,1)S(1)} %collective-permute-done.other_ref), custom_call_target="tpu_custom_call" | custom-call | tf_op jit(solution)/shard_map/attend/pallas_call | solution.py:359
Async XLA Ops:
  0.0 59.1 %copy-start.2 = (s32[1,16]{1,0:T(1,128)S(1)}, s32[1,16]{1,0:T(1,128)}, u32[]{:S(2)}) copy-start(s32[1,16]{1,0:T(1,128)} %mask_ref.1) | copy-start | bytes 196
  57.1 4.1 %collective-permute-start = (bf16[16,192,128]{2,1,0:T(8,128)(2,1)S(1)}, bf16[16,192,128]{2,1,0:T(8,128)(2,1)S(1)}, u32[]{:S(2)}, u32[]{:S(2)}) collective-permute-start(bf16[16,192,128]{2,1,0:T(8,128)(2,1)S(1)} %all_to_all.11.mine_ref), channel_id=1, source_target_pairs={{0,1},{1,0},{2,3},{3,2},{4,5},{5,4},{6,7},{7,6},{8,9},{9,8},{10,11... | collective-permute-start | bytes 2359304 | tf_op jit(solution)/shard_map/ppermute | solution.py:346
  59.1 0.8 %copy-start.1 = (bf16[2,128,128]{2,1,0:T(8,128)(2,1)S(1)}, bf16[2,128,128]{2,1,0:T(8,128)(2,1)}, u32[]{:S(2)}) copy-start(bf16[2,128,128]{2,1,0:T(8,128)(2,1)} %get-tuple-element.12.q_ref) | copy-start | bytes 196612
  61.2 0.8 %copy-start = (f32[128,128]{1,0:T(8,128)S(1)}, f32[128,128]{1,0:T(8,128)}, u32[]{:S(2)}) copy-start(f32[128,128]{1,0:T(8,128)} %get-tuple-element.18.start_ref) | copy-start | bytes 196612

commit v2 on v1

--- a/solution.py
+++ b/solution.py
@@ -52,8 +52,8 @@
 
 def project_kernel(
     x_hbm, img_hbm, wq_hbm, wk_hbm, wv_hbm, gain_hbm, bq_hbm, bv_hbm, dest_hbm, invf_hbm, docs_ref,
-    q_ref, kv_ref, tail_hbm, cs_hbm, start_hbm,
-    xs, wqs, wkvs, gains, bqs, bvs, dests, invfs, tails, css, starts, sems, small_sems, out_sems,
+    q_hbm, kv_hbm, tail_hbm, cs_hbm, start_hbm,
+    q_ref, kv_ref, xs, wqs, wkvs, gains, bqs, bvs, dests, invfs, tails, css, starts, sems, small_sems, out_sems,
 ):
     width = xs.shape[1]
     step = width // KCH
@@ -124,7 +124,9 @@
     outs = [
         pltpu.make_async_copy(css, cs_hbm, out_sems.at[0]),
         pltpu.make_async_copy(starts, start_hbm, out_sems.at[1]),
-        pltpu.make_async_copy(tails, tail_hbm, out_sems.at[2]),
+        pltpu.make_async_copy(kv_ref, kv_hbm, out_sems.at[2]),
+        pltpu.make_async_copy(q_ref, q_hbm, out_sems.at[3]),
+        pltpu.make_async_copy(tails, tail_hbm, out_sems.at[4]),
     ]
     outs[0].start()
     outs[1].start()
@@ -145,8 +147,9 @@
         copy.wait()
     queries = jnp.broadcast_to(bqs[...].astype(f32).reshape(1, 2 * HD), (ROWS, 2 * HD))
     kv = jnp.zeros((ROWS, 64), f32)
+    for copy in copies[4:]:
+        copy.wait()
     for c in range(KCH):
-        copies[4 + c].wait()
         part = pl.ds(c * step, step)
         gain = gains[part].astype(f32).reshape(1, step)
         normed = (xs[:, part].astype(f32) * inverse * gain).astype(bf16)
@@ -165,6 +168,7 @@
         for j in range(2):
             kv_ref[4 * g + 2 * j] = key
             kv_ref[4 * g + 2 * j + 1] = value
+    outs[2].start()
 
     cosine = css[0]
     sine = css[1]
@@ -176,8 +180,9 @@
         tail = tail + jnp.dot(
             jnp.where(pick, 1.0, 0.0).astype(bf16), v[TOK:], preferred_element_type=f32
         )
+    outs[3].start()
     tails[...] = tail.astype(bf16).reshape(N_SEQ, TAIL, HD)
-    outs[2].start()
+    outs[4].start()
     for out in outs:
         out.wait()
 
@@ -193,7 +198,8 @@
         pay_ref[p, ROWS:PAY, :] = tail_ref[p]
 
 
-def place_kernel(q_ref, mine_ref, mask_ref, merged_ref, where_ref):
+def place_kernel(q_ref, mine_ref, first_ref, mask_ref, merged_ref, where_ref, start_ref):
+    start_ref[...] = first_ref[...]
     tails = mine_ref[:, ROWS:PAY, :].astype(f32)
     hi_all = tails[:, 12, :]
     lo_all = tails[:, 13, :]
@@ -280,6 +286,54 @@
     return pl.BlockSpec(memory_space=pltpu.VMEM)
 
 
+def project_call(width):
+    hbm = pl.BlockSpec(memory_space=pltpu.HBM)
+    smem = pl.BlockSpec(memory_space=pltpu.SMEM)
+    return pl.pallas_call(
+        project_kernel,
+        name="project",
+        out_shape=(
+            jax.ShapeDtypeStruct((2, TOK, HD), bf16),
+            jax.ShapeDtypeStruct((N_HEAD, 8, 256), bf16),
+            jax.ShapeDtypeStruct((N_SEQ, TAIL, HD), bf16),
+            jax.ShapeDtypeStruct((2, ROWS, HD), f32),
+            jax.ShapeDtypeStruct((TOK, HD), f32),
+        ),
+        in_specs=[hbm] * 10 + [smem],
+        out_specs=(hbm,) * 5,
+        scratch_shapes=[
+            pltpu.VMEM((2, TOK, HD), bf16),
+            pltpu.VMEM((N_HEAD, 8, 256), bf16),
+            pltpu.VMEM((ROWS, width), bf16),
+            pltpu.VMEM((width, 2 * HD), bf16),
+            pltpu.VMEM((64, width), bf16),
+            pltpu.VMEM((width,), bf16),
+            pltpu.VMEM((2 * HD,), bf16),
+            pltpu.VMEM((4, 8), bf16),
+            pltpu.VMEM((1, IMG), jnp.int32),
+            pltpu.VMEM((1, HD), f32),
+            pltpu.VMEM((N_SEQ, TAIL, HD), bf16),
+            pltpu.VMEM((2, ROWS, HD), f32),
+            pltpu.VMEM((TOK, HD), f32),
+            pltpu.SemaphoreType.DMA((4 + KCH,)),
+            pltpu.SemaphoreType.DMA((5,)),
+            pltpu.SemaphoreType.DMA((5,)),
+        ],
+        compiler_params=pltpu.CompilerParams(vmem_limit_bytes=LIMIT),
+    )
+
+
+def panel_call():
+    return pl.pallas_call(
+        panel_kernel,
+        name="panel",
+        out_shape=jax.ShapeDtypeStruct((N_SEQ, PAY, HD), bf16),
+        in_specs=[vmem()] * 3,
+        out_specs=vmem(),
+        compiler_params=pltpu.CompilerParams(vmem_limit_bytes=SMALL),
+    )
+
+
 def body(
     embedded,
     norm_gain,
@@ -296,66 +350,30 @@
     width = embedded.shape[1]
     half = np.arange(HD) % (HD // 2)
     inverse = jnp.asarray((rope_base ** (-2.0 * half / HD)).astype(np.float32)[None, :])
-    hbm = pl.BlockSpec(memory_space=pltpu.HBM)
     smem = pl.BlockSpec(memory_space=pltpu.SMEM)
     key_t = jnp.transpose(key_weight, (1, 2, 0)).reshape(32, width)
     value_t = jnp.transpose(value_weight, (1, 2, 0)).reshape(32, width)
-    queries, kv_send, tail, tables, start = pl.pallas_call(
-        project_kernel,
-        name="project",
-        out_shape=(
-            jax.ShapeDtypeStruct((2, TOK, HD), bf16),
-            jax.ShapeDtypeStruct((N_HEAD, 8, 256), bf16),
-            jax.ShapeDtypeStruct((N_SEQ, TAIL, HD), bf16),
-            jax.ShapeDtypeStruct((2, ROWS, HD), f32),
-            jax.ShapeDtypeStruct((TOK, HD), f32),
-        ),
-        in_specs=[hbm] * 10 + [smem],
-        out_specs=(vmem(), vmem(), hbm, hbm, hbm),
-        scratch_shapes=[
-            pltpu.VMEM((ROWS, width), bf16),
-            pltpu.VMEM((width, 2 * HD), bf16),
-            pltpu.VMEM((64, width), bf16),
-            pltpu.VMEM((width,), bf16),
-            pltpu.VMEM((2 * HD,), bf16),
-            pltpu.VMEM((4, 8), bf16),
-            pltpu.VMEM((1, IMG), jnp.int32),
-            pltpu.VMEM((1, HD), f32),
-            pltpu.VMEM((N_SEQ, TAIL, HD), bf16),
-            pltpu.VMEM((2, ROWS, HD), f32),
-            pltpu.VMEM((TOK, HD), f32),
-            pltpu.SemaphoreType.DMA((4 + KCH,)),
-            pltpu.SemaphoreType.DMA((5,)),
-            pltpu.SemaphoreType.DMA((3,)),
-        ],
-        compiler_params=pltpu.CompilerParams(vmem_limit_bytes=LIMIT),
-    )(
+    queries, kv_send, tail, tables, start = project_call(width)(
         embedded, image_rows, query_weight, key_t, value_t, norm_gain, query_bias,
         value_bias, image_dest[None, :], inverse, doc_lengths,
     )
     kv_mine = lax.all_to_all(kv_send, "head", 0, 0)
-    payload = pl.pallas_call(
-        panel_kernel,
-        name="panel",
-        out_shape=jax.ShapeDtypeStruct((N_SEQ, PAY, HD), bf16),
-        in_specs=[vmem()] * 3,
-        out_specs=vmem(),
-        compiler_params=pltpu.CompilerParams(vmem_limit_bytes=LIMIT),
-    )(kv_mine, tables, tail)
+    payload = panel_call()(kv_mine, tables, tail)
     mine = lax.all_to_all(payload, "seq", 0, 0)
     other = lax.ppermute(mine, "head", [(i, i ^ 1) for i in range(N_HEAD)])
-    merged, where = pl.pallas_call(
+    merged, where, start = pl.pallas_call(
         place_kernel,
         name="place",
         out_shape=(
             jax.ShapeDtypeStruct((2 * TOK, HD), bf16),
             jax.ShapeDtypeStruct((N_SEQ + N_SEQ // 2, HD), f32),
+            jax.ShapeDtypeStruct((TOK, HD), f32),
         ),
-        in_specs=[vmem(), vmem(), smem],
-        out_specs=(vmem(), vmem()),
+        in_specs=[vmem()] * 3 + [smem],
+        out_specs=(vmem(),) * 3,
         compiler_params=pltpu.CompilerParams(vmem_limit_bytes=SMALL),
         cost_estimate=pl.CostEstimate(flops=1 << 28, bytes_accessed=1 << 20, transcendentals=0),
-    )(queries, mine, block_mask)
+    )(queries, mine, start, block_mask)
     return pl.pallas_call(
         attend_kernel,
         name="attend",

time: 65.3 us -> 63.9 us (0.979)
  Pallas kernels: 14.2 us -> 11.3 us
  local copies, waits for them, and re-layouts: 1.68 us -> 3.44 us
    pallas_call x2, Pallas kernels: 10 us -> 7.11 us  [the longest x1 6.9 us: body(): project_call(width)]
    unnamed x6 -> x10, local copies, waits for them, and re-layouts: 1.68 us -> 3.44 us
where the time goes in v2:
time: 63.9 us; the launch traced here: 63.6 us
  blocking collectives  46.7 us (73%)
  Pallas kernels  11.3 us (18%)
  local copies, waits for them, and re-layouts  3.44 us (5%)
  starting transfers between devices  2.05 us (3%)
    all_to_all x1, blocking collectives, body(): mine = lax.all_to_all(payload, 'seq', 0, 0)  34 us
    all_to_all x1, blocking collectives, body(): kv_mine = lax.all_to_all(kv_send, 'head', 0, 0)  12.7 us
    pallas_call x1, Pallas kernels, body(): project_call(width)  6.9 us
    unnamed x10, local copies, waits for them, and re-layouts  3.44 us
    pallas_call x1, Pallas kernels, body(): pl.pallas_call(attend_kernel, name='attend', out_shape=jax.ShapeDtypeStru...  2.98 us
    ppermute x1, starting transfers between devices, body(): other = lax.ppermute(mine, 'head', [(i, i ^ 1) for i in range(N_HEAD)])  2.05 us
  transfers between devices with their start and end apart: 1, of which 0 were waited for; matrix products, arithmetic and copies ran while one was open for 0% of the time, Pallas kernels for 2%

profile of v2, /device:TPU:1, one launch (start us, length us, event | category | flops | bytes accessed | tf_op | source)
XLA Modules:
  0.0 63.6 jit_solution(16639740538587491541)
XLA Ops:
  0.0 0.0 copy-start.4
  0.0 6.9 %project.1 = (bf16[2,128,128]{2,1,0:T(8,128)(2,1)}, bf16[16,8,256]{2,1,0:T(8,128)(2,1)}, bf16[16,16,128]{2,1,0:T(8,128)(2,1)}, f32[2,176,128]{2,1,0:T(8,128)}, f32[128,128]{1,0:T(8,128)}) custom-call(bf16[128,8192]{1,0:T(8,128)(2,1)} %x_hbm.1, bf16[48,8192]{1,0:T(8,128)(2,1)} %img_hbm.1, bf16[8192,256]{1,0:T(8,128)(2,1)} %wq_hbm.1, ...), custom_call_target="tpu_custom_call" | custom-call | tf_op jit(solution)/shard_map/project/pallas_call | solution.py:356
  6.9 12.7 %all_to_all.10.kv_ref = bf16[16,8,256]{2,1,0:T(8,128)(2,1)S(1)} all-to-all(bf16[16,8,256]{2,1,0:T(8,128)(2,1)} %get-tuple-element.14), channel_id=1, replica_groups=mesh['seq'=16,'head'=16] {'head'}, dimensions={0} | all-to-all | bytes 131072 | tf_op jit(solution)/shard_map/all_to_all | solution.py:360
  19.7 0.0 copy-start
  19.7 0.9 %copy-done = f32[2,176,128]{2,1,0:T(8,128)S(1)} copy-done((f32[2,176,128]{2,1,0:T(8,128)S(1)}, f32[2,176,128]{2,1,0:T(8,128)}, u32[]{:S(2)}) %copy-start) | copy-done | bytes 180248
  20.6 0.0 copy-start.1
  20.6 0.8 %copy-done.1 = bf16[16,16,128]{2,1,0:T(8,128)(2,1)S(1)} copy-done((bf16[16,16,128]{2,1,0:T(8,128)(2,1)S(1)}, bf16[16,16,128]{2,1,0:T(8,128)(2,1)}, u32[]{:S(2)}) %copy-start.1) | copy-done | bytes 65560
  21.4 0.2 panel.1
  21.6 34.0 %all_to_all.11.mine_ref = bf16[16,192,128]{2,1,0:T(8,128)(2,1)S(1)} all-to-all(bf16[16,192,128]{2,1,0:T(8,128)(2,1)S(1)} %panel.1), channel_id=1, replica_groups=mesh['seq'=16,'head'=16] {'seq'}, dimensions={0} | all-to-all | bytes 1572864 | tf_op jit(solution)/shard_map/all_to_all | solution.py:362
  55.6 2.0 %collective-permute-start = (bf16[16,192,128]{2,1,0:T(8,128)(2,1)S(1)}, bf16[16,192,128]{2,1,0:T(8,128)(2,1)S(1)}, u32[]{:S(2)}, u32[]{:S(2)}) collective-permute-start(bf16[16,192,128]{2,1,0:T(8,128)(2,1)S(1)} %all_to_all.11.mine_ref), channel_id=1, source_target_pairs={{0,1},{1,0},{2,3},{3,2},{4,5},{5,4},{6,7},{7,6},{8,9},{9,8},{10,11... | collective-permute-start | bytes 2359304 | tf_op jit(solution)/shard_map/ppermute | solution.py:363
  57.7 0.0 copy-done.4
  57.7 0.0 copy-start.2
  57.7 0.8 %copy-done.2 = bf16[2,128,128]{2,1,0:T(8,128)(2,1)S(1)} copy-done((bf16[2,128,128]{2,1,0:T(8,128)(2,1)S(1)}, bf16[2,128,128]{2,1,0:T(8,128)(2,1)}, u32[]{:S(2)}) %copy-start.2) | copy-done | bytes 65560
  58.5 0.0 copy-start.3
  58.5 0.8 %copy-done.3 = f32[128,128]{1,0:T(8,128)S(1)} copy-done((f32[128,128]{1,0:T(8,128)S(1)}, f32[128,128]{1,0:T(8,128)}, u32[]{:S(2)}) %copy-start.3) | copy-done | bytes 65560
  59.4 1.2 %place.1 = (bf16[256,128]{1,0:T(8,128)(2,1)S(1)}, f32[24,128]{1,0:T(8,128)S(1)}, f32[128,128]{1,0:T(8,128)S(1)}) custom-call(bf16[2,128,128]{2,1,0:T(8,128)(2,1)S(1)} %copy-done.2, bf16[16,192,128]{2,1,0:T(8,128)(2,1)S(1)} %all_to_all.11.mine_ref, f32[128,128]{1,0:T(8,128)S(1)} %copy-done.3, s32[1,16]{1,0:T(1,128)S(1)} %copy-done.4), custom_call_target="tpu_custom_call" | custom-call | flops 268435456 | bytes 1048576 | tf_op jit(solution)/shard_map/place/pallas_call | solution.py:364
  60.6 0.0 collective-permute-done.other_ref
  60.6 3.0 %attend.1 = bf16[128,256]{1,0:T(8,128)(2,1)} custom-call(bf16[256,128]{1,0:T(8,128)(2,1)S(1)} %get-tuple-element.18.q_ref, f32[24,128]{1,0:T(8,128)S(1)} %get-tuple-element.19.where_ref, f32[128,128]{1,0:T(8,128)S(1)} %get-tuple-element.20.start_ref, bf16[16,192,128]{2,1,0:T(8,128)(2,1)S(1)} %all_to_all.11.mine_ref, ...), custom_call_target="tpu_custom_call" | custom-call | tf_op jit(solution)/shard_map/attend/pallas_call | solution.py:377
Async XLA Ops:
  0.0 57.7 %copy-start.4 = (s32[1,16]{1,0:T(1,128)S(1)}, s32[1,16]{1,0:T(1,128)}, u32[]{:S(2)}) copy-start(s32[1,16]{1,0:T(1,128)} %mask_ref.1) | copy-start | bytes 196
  19.7 0.9 %copy-start = (f32[2,176,128]{2,1,0:T(8,128)S(1)}, f32[2,176,128]{2,1,0:T(8,128)}, u32[]{:S(2)}) copy-start(f32[2,176,128]{2,1,0:T(8,128)} %get-tuple-element.15.cs_ref) | copy-start | bytes 540676
  20.6 0.8 %copy-start.1 = (bf16[16,16,128]{2,1,0:T(8,128)(2,1)S(1)}, bf16[16,16,128]{2,1,0:T(8,128)(2,1)}, u32[]{:S(2)}) copy-start(bf16[16,16,128]{2,1,0:T(8,128)(2,1)} %get-tuple-element.16.tail_ref) | copy-start | bytes 196612
  55.6 4.9 %collective-permute-start = (bf16[16,192,128]{2,1,0:T(8,128)(2,1)S(1)}, bf16[16,192,128]{2,1,0:T(8,128)(2,1)S(1)}, u32[]{:S(2)}, u32[]{:S(2)}) collective-permute-start(bf16[16,192,128]{2,1,0:T(8,128)(2,1)S(1)} %all_to_all.11.mine_ref), channel_id=1, source_target_pairs={{0,1},{1,0},{2,3},{3,2},{4,5},{5,4},{6,7},{7,6},{8,9},{9,8},{10,11... | collective-permute-start | bytes 2359304 | tf_op jit(solution)/shard_map/ppermute | solution.py:363
  57.7 0.8 %copy-start.2 = (bf16[2,128,128]{2,1,0:T(8,128)(2,1)S(1)}, bf16[2,128,128]{2,1,0:T(8,128)(2,1)}, u32[]{:S(2)}) copy-start(bf16[2,128,128]{2,1,0:T(8,128)(2,1)} %get-tuple-element.13.q_ref) | copy-start | bytes 196612
  58.5 0.8 %copy-start.3 = (f32[128,128]{1,0:T(8,128)S(1)}, f32[128,128]{1,0:T(8,128)}, u32[]{:S(2)}) copy-start(f32[128,128]{1,0:T(8,128)} %get-tuple-element.17.first_ref) | copy-start | bytes 196612

commit v3 on v2

v3 whole, which is shorter than its diff:
```python
import functools
import math

import jax
import jax.numpy as jnp
import numpy as np
from jax import lax
from jax.experimental import pallas as pl
from jax.experimental.pallas import tpu as pltpu
from jax.sharding import PartitionSpec as P

HD = 128
GROUP = 8
BLK = 128
CAP = 6
TOK = 128
IMG = 48
N_SEQ = 16
N_HEAD = 16
ROWS = TOK + IMG
HALF_TOK = TOK // 2
HALF_IMG = IMG // 2
KEYS = HALF_TOK + HALF_IMG
TAIL = 16
PAY = KEYS + 2 * TAIL
TILES = N_SEQ // 2 + N_SEQ // 4
DOCS = 32
KCH = 4
LIMIT = 60 << 20
SMALL = 12 << 20

rope_base = 1000000.0
norm_eps = 1e-06
BIG = 1.0e6
NEG = -1.0e30
LOW = -1.0e29

f32 = jnp.float32
bf16 = jnp.bfloat16


def iota(shape, dim):
    return lax.broadcasted_iota(jnp.int32, shape, dim)


def fiota(shape, dim):
    return iota(shape, dim).astype(f32)


def dot_t(a, b):
    return lax.dot_general(a, b, (((1,), (1,)), ((), ())), preferred_element_type=f32)


def tdot(a, b):
    return lax.dot_general(a, b, (((0,), (0,)), ((), ())), preferred_element_type=f32)


def project_kernel(
    x_hbm, img_hbm, wq_hbm, wk_hbm, wv_hbm, gain_hbm, bq_hbm, bv_hbm, dest_hbm, invf_hbm, docs_ref,
    kv_hbm, share_hbm, aux_hbm, own_hbm,
    kv_ref, share, aux, own, xs, wqs, wkvs, gains, bqs, bvs, dests, invfs, css, sems, small_sems, out_sems,
):
    width = xs.shape[1]
    step = width // KCH
    copies = [
        pltpu.make_async_copy(x_hbm, xs.at[pl.ds(0, TOK)], sems.at[0]),
        pltpu.make_async_copy(img_hbm, xs.at[pl.ds(TOK, IMG)], sems.at[1]),
        pltpu.make_async_copy(wk_hbm, wkvs.at[pl.ds(0, 32)], sems.at[2]),
        pltpu.make_async_copy(wv_hbm, wkvs.at[pl.ds(32, 32)], sems.at[3]),
    ]
    for c in range(KCH):
        part = pl.ds(c * step, step)
        copies.append(pltpu.make_async_copy(wq_hbm.at[part], wqs.at[part], sems.at[4 + c]))
    small = [
        pltpu.make_async_copy(src, dst, small_sems.at[i])
        for i, (src, dst) in enumerate(
            ((dest_hbm, dests), (invf_hbm, invfs), (gain_hbm, gains), (bq_hbm, bqs), (bv_hbm, bvs))
        )
    ]
    for copy in small[:2] + copies[:2] + small[2:] + copies[2:]:
        copy.start()
    small[0].wait()
    small[1].wait()

    seq_place = lax.axis_index("seq")
    first = (seq_place * TOK).astype(f32)
    dest_row = dests[...].astype(f32)
    eye = iota((IMG, IMG), 0) == iota((IMG, IMG), 1)
    dest_col = jnp.sum(jnp.where(eye, dest_row, 0.0), axis=1, keepdims=True)
    hi_row = jnp.floor(dest_row * (1.0 / TOK))
    hi_col = jnp.floor(dest_col * (1.0 / TOK))
    lo_row = dest_row - TOK * hi_row
    lo_col = dest_col - TOK * hi_col

    index_col = jnp.concatenate([first + fiota((TOK, 1), 0), dest_col], axis=0)
    start_col = jnp.zeros((ROWS, 1), f32)
    begin = jnp.int32(0)
    for d in range(DOCS):
        begin_f = begin.astype(f32)
        start_col = jnp.where(index_col >= begin_f, begin_f, start_col)
        begin = begin + docs_ref[d]
    own[2 * TOK :, :] = jnp.broadcast_to(start_col[:TOK], (TOK, HD))
    angles = (index_col - start_col) * invfs[...]
    cosine = jnp.cos(angles)
    sine = jnp.sin(angles)
    sine = jnp.where(iota((ROWS, HD), 1) < HD // 2, -sine, sine)
    upper = (lax.axis_index("head") // 2) % 2 == 1
    for i, table in enumerate((cosine, sine)):
        css[i] = table
        low = i * KEYS
        aux[low : low + HALF_TOK, :] = jnp.where(upper, table[HALF_TOK:TOK], table[:HALF_TOK])
        aux[low + HALF_TOK : low + KEYS, :] = jnp.where(
            upper, table[TOK + HALF_IMG :], table[TOK : TOK + HALF_IMG]
        )

    earlier = iota((IMG, IMG), 0) < iota((IMG, IMG), 1)
    later = iota((IMG, IMG), 0) > iota((IMG, IMG), 1)
    same = hi_col == hi_row
    rank_row = jnp.sum(jnp.where(same & earlier, 1.0, 0.0), axis=0, keepdims=True)
    rank_col = jnp.sum(jnp.where(same & later, 1.0, 0.0), axis=1, keepdims=True)
    count = N_SEQ * TAIL
    line = iota((count, IMG), 0)
    here = hi_row == (line // TAIL).astype(f32)
    slot = (line % TAIL).astype(f32)
    offsets = jnp.where(here & (slot == 14.0), lo_row + 1.0, 0.0).astype(bf16)
    lane = iota((IMG, HD), 1)
    ranked = jnp.where((rank_col == lane.astype(f32)) & (lane < CAP), 1.0, 0.0).astype(bf16)
    tail = jnp.dot(offsets, ranked, preferred_element_type=f32)
    skip = jnp.where(upper, HALF_IMG, 0)
    spread = (lane % 32 + skip == iota((IMG, HD), 0)) & (lane % 32 < HALF_IMG)
    unused = (iota((1, HD), 1) % 32) >= HALF_IMG
    hi_two = jnp.where(unused, 99.0, jnp.sum(jnp.where(spread, hi_col, 0.0), axis=0, keepdims=True))
    lo_two = jnp.sum(jnp.where(spread, lo_col, 0.0), axis=0, keepdims=True)
    wide_slot = iota((count, HD), 0) % TAIL
    tail = tail + jnp.where(wide_slot == 12, hi_two, jnp.where(wide_slot == 13, lo_two, 0.0))

    outs = [
        pltpu.make_async_copy(kv_ref, kv_hbm, out_sems.at[0]),
        pltpu.make_async_copy(share, share_hbm, out_sems.at[1]),
        pltpu.make_async_copy(own, own_hbm, out_sems.at[2]),
        pltpu.make_async_copy(aux, aux_hbm, out_sems.at[3]),
    ]

    inverse = []
    for i, rows in enumerate((pl.ds(0, TOK), pl.ds(TOK, IMG))):
        copies[i].wait()
        squares = jnp.zeros((rows.size, HD), f32)
        for c in range(width // HD):
            wide = xs[rows, c * HD : (c + 1) * HD].astype(f32)
            squares = squares + wide * wide
        inverse.append(
            lax.rsqrt(jnp.sum(squares, axis=1, keepdims=True) * (1.0 / width) + norm_eps)
        )
    inverse = jnp.concatenate(inverse, axis=0)

    for copy in small[2:] + copies[2:4]:
        copy.wait()
    queries = jnp.broadcast_to(bqs[...].astype(f32).reshape(1, 2 * HD), (ROWS, 2 * HD))
    kv = jnp.zeros((ROWS, 64), f32)
    for copy in copies[4:]:
        copy.wait()
    for c in range(KCH):
        part = pl.ds(c * step, step)
        gain = gains[part].astype(f32).reshape(1, step)
        normed = (xs[:, part].astype(f32) * inverse * gain).astype(bf16)
        kv = kv + dot_t(normed, wkvs[:, part])
        queries = queries + jnp.dot(normed, wqs[part, :], preferred_element_type=f32)

    kv = jnp.concatenate([kv, jnp.zeros((ROWS, 64), f32)], axis=1)
    eye8 = iota((8, 8), 0) == iota((8, 8), 1)
    for j in range(2):
        kv_t = jnp.transpose(
            jnp.concatenate(
                [
                    kv[HALF_TOK * j : HALF_TOK * (j + 1)],
                    kv[TOK + HALF_IMG * j : TOK + HALF_IMG * (j + 1)],
                    jnp.zeros((HD - KEYS, HD), f32),
                ],
                axis=0,
            )
        )
        for g in range(4):
            bias_row = bvs[g : g + 1, :].astype(f32)
            bias = jnp.sum(jnp.where(eye8, bias_row, 0.0), axis=1, keepdims=True)
            kv_ref[4 * g + 2 * j] = kv_t[8 * g : 8 * g + 8].astype(bf16)
            kv_ref[4 * g + 2 * j + 1] = (kv_t[32 + 8 * g : 40 + 8 * g] + bias).astype(bf16)
    outs[0].start()

    cosine = css[0]
    sine = css[1]
    for e in range(2):
        v = queries[:, e * HD : (e + 1) * HD]
        v = (v * cosine + pltpu.roll(v, HD // 2, 1) * sine).astype(bf16)
        share[e * TOK : (e + 1) * TOK, :] = v[:TOK]
        own[e * TOK : (e + 1) * TOK, :] = v[:TOK].astype(f32)
        pick = here & (rank_row == slot - CAP * e) & (slot >= CAP * e) & (slot < CAP * e + CAP)
        tail = tail + jnp.dot(
            jnp.where(pick, 1.0, 0.0).astype(bf16), v[TOK:], preferred_element_type=f32
        )
    outs[2].start()
    share[2 * TOK :, :] = tail.astype(bf16)
    outs[1].start()
    aux[2 * KEYS :, :] = tail
    outs[3].start()
    for out in outs:
        out.wait()


def panel_kernel(kv_ref, aux_ref, share_ref, pay_ref):
    is_key = lax.axis_index("head") % 2 == 0
    panel = jnp.transpose(kv_ref[...].astype(f32).reshape(HD, HD))[:KEYS]
    cosine = jnp.where(is_key, aux_ref[0:KEYS, :], 1.0)
    sine = jnp.where(is_key, aux_ref[KEYS : 2 * KEYS, :], 0.0)
    panel = (panel * cosine + pltpu.roll(panel, HD // 2, 1) * sine).astype(bf16)
    for p in range(N_SEQ):
        low = 2 * KEYS + TAIL * p
        pay_ref[p, 0:KEYS, :] = panel
        pay_ref[p, KEYS : KEYS + TAIL, :] = aux_ref[low : low + TAIL, :].astype(bf16)
        low = 2 * TOK + TAIL * p
        pay_ref[p, KEYS + TAIL : PAY, :] = share_ref[low : low + TAIL, :]


def place_kernel(own_ref, share_ref, mine_ref, mask_ref, merged_ref, where_ref, start_ref):
    start_ref[...] = own_ref[2 * TOK :, :]
    tails = mine_ref[:, KEYS:PAY, :].astype(f32)
    slots = tails[:, 14, :]
    count = N_SEQ * TAIL
    owner = iota((count, N_SEQ), 0) // TAIL == iota((count, N_SEQ), 1)
    spread = jnp.dot(
        jnp.where(owner, 1.0, 0.0).astype(bf16), slots.astype(bf16), preferred_element_type=f32
    )
    line = iota((count, HD), 0) % TAIL
    lane = iota((count, HD), 1)
    flats = [tails[:, c * TAIL : (c + 1) * TAIL, :].reshape(count, HD).astype(bf16) for c in range(2)]
    for e in range(2):
        slot = line - CAP * e
        used = (slot >= 0) & (slot < CAP)
        offset = jnp.sum(jnp.where(used & (lane == slot), spread, 0.0), axis=1, keepdims=True)
        place = jnp.where(offset == lane.astype(f32) + 1.0, 1.0, 0.0).astype(bf16)
        taken = tdot(place, jnp.ones((count, HD), bf16)) > 0.5
        span = slice(e * TOK, (e + 1) * TOK)
        merged_ref[span, :] = jnp.where(taken, tdot(place, flats[0]), own_ref[span, :]).astype(bf16)
        moved = jnp.where(taken, tdot(place, flats[1]), share_ref[span, :].astype(f32))
        merged_ref[(2 + e) * TOK : (3 + e) * TOK, :] = moved.astype(bf16)

    lane = iota((1, HD), 1)

    def four(rows, m):
        row = rows[4 * m + 3 : 4 * m + 4]
        for i in (2, 1, 0):
            row = jnp.where(lane < 32 * (i + 1), rows[4 * m + i : 4 * m + i + 1], row)
        return row

    covered = jnp.zeros((N_SEQ, HD), f32)
    for c in range(2):
        hi_all = tails[:, c * TAIL + 12, :]
        lo_all = tails[:, c * TAIL + 13, :]
        for m in range(N_SEQ // 4):
            hi = four(hi_all, m)
            lo = four(lo_all, m)
            hi_hot = jnp.where(hi == fiota((N_SEQ, HD), 0), 1.0, 0.0).astype(bf16)
            lo_hot = jnp.where(lo == fiota((HD, HD), 0), 1.0, 0.0).astype(bf16)
            covered = covered + dot_t(hi_hot, lo_hot)
            if c == 0:
                seen = jnp.zeros((1, HD), f32)
                for b in range(N_SEQ):
                    seen = jnp.where(hi == float(b), mask_ref[0, b].astype(f32), seen)
                at = N_SEQ // 2 + m
                where_ref[at : at + 1, :] = jnp.where(seen > 0.5, hi * float(TOK) + lo, BIG)
    upper = (lax.axis_index("head") // 2) % 2 == 1
    turned = pltpu.roll(covered, HALF_TOK, 1)
    near = jnp.where(upper, turned, covered)
    far = jnp.where(upper, covered, turned)
    base = (lane % HALF_TOK).astype(f32) + jnp.where(upper, float(HALF_TOK), 0.0)
    for m in range(N_SEQ // 2):
        left = lane < HALF_TOK
        taken = jnp.where(left, near[2 * m : 2 * m + 1], far[2 * m + 1 : 2 * m + 2])
        seen = jnp.where(left, mask_ref[0, 2 * m], mask_ref[0, 2 * m + 1])
        position = base + jnp.where(left, float(TOK * 2 * m), float(TOK * (2 * m + 1)))
        where_ref[m : m + 1, :] = jnp.where((taken < 0.5) & (seen == 1), position, BIG)


def attend_kernel(q_ref, where_ref, start_ref, mine_ref, other_ref, keep_ref, send_ref, scores):
    is_key = lax.axis_index("head") % 2 == 0
    first = (lax.axis_index("seq") * TOK).astype(f32)
    slope = math.log2(math.e) / math.sqrt(HD)

    def tile_of(ref, t):
        if t < N_SEQ // 2:
            return ref[2 * t : 2 * t + 2, 0:HALF_TOK, :].reshape(HD, HD)
        m = t - N_SEQ // 2
        return ref[4 * m : 4 * m + 4, HALF_TOK : HALF_TOK + 32, :].reshape(HD, HD)

    def attend(keys, values):
        queries = q_ref[...]
        position = first + fiota((TOK, HD), 0)
        start = start_ref[...]
        top = jnp.full((4 * TOK, HD), NEG, f32)
        for t in range(TILES):
            where = where_ref[t : t + 1, :]
            allowed = (where <= position) & (where >= start)
            allowed = jnp.concatenate([allowed] * 4, axis=0)
            score = jnp.where(allowed, dot_t(queries, tile_of(keys, t)), NEG)
            scores[t] = score
            top = jnp.maximum(top, score)
        top = jnp.maximum(jnp.max(top, axis=1, keepdims=True), LOW)
        total = jnp.zeros((4 * TOK, HD), f32)
        mix = jnp.zeros((4 * TOK, HD), f32)
        for t in range(TILES):
            weight = jnp.exp2((scores[t] - top) * slope)
            total = total + weight
            mix = mix + jnp.dot(weight.astype(bf16), tile_of(values, t), preferred_element_type=f32)
        total = jnp.sum(total, axis=1, keepdims=True)
        mine = 2 * TOK
        keep_ref[0] = mix[:mine]
        keep_ref[1] = jnp.broadcast_to(top[:mine], (mine, HD))
        keep_ref[2] = jnp.broadcast_to(total[:mine], (mine, HD))
        send_ref[0:mine, :] = (mix[mine:] / jnp.maximum(total[mine:], 1.0e-30)).astype(bf16)
        rows = []
        for column in (top[mine:], total[mine:]):
            for e in range(2):
                part = jnp.broadcast_to(column[e * TOK : (e + 1) * TOK], (TOK, HD))
                left = jnp.transpose(part)[0:1]
                for _ in range(3):
                    piece = left.astype(bf16).astype(f32)
                    rows.append(piece)
                    left = left - piece
        rows.append(jnp.zeros((4, HD), f32))
        send_ref[mine:, :] = jnp.concatenate(rows, axis=0).astype(bf16)

    @pl.when(is_key)
    def _():
        attend(mine_ref, other_ref)

    @pl.when(jnp.logical_not(is_key))
    def _():
        attend(other_ref, mine_ref)


def combine_kernel(keep_ref, come_ref, out_ref):
    slope = math.log2(math.e) / math.sqrt(HD)
    pieces = come_ref[2 * TOK :, :].astype(f32)

    def column(i):
        row = pieces[3 * i : 3 * i + 1] + pieces[3 * i + 1 : 3 * i + 2] + pieces[3 * i + 2 : 3 * i + 3]
        return jnp.transpose(jnp.broadcast_to(row, (TOK, HD)))

    for e in range(2):
        span = slice(e * TOK, (e + 1) * TOK)
        top_near = keep_ref[1, span, :]
        top_far = column(e)
        top = jnp.maximum(top_near, top_far)
        near = jnp.exp2((top_near - top) * slope)
        far = jnp.exp2((top_far - top) * slope) * column(2 + e)
        mix = keep_ref[0, span, :] * near + come_ref[span, :].astype(f32) * far
        out_ref[:, e * HD : (e + 1) * HD] = (mix / (keep_ref[2, span, :] * near + far)).astype(bf16)


def vmem():
    return pl.BlockSpec(memory_space=pltpu.VMEM)


def small_params():
    return pltpu.CompilerParams(vmem_limit_bytes=SMALL)


def project_call(width):
    hbm = pl.BlockSpec(memory_space=pltpu.HBM)
    smem = pl.BlockSpec(memory_space=pltpu.SMEM)
    outputs = [
        ((N_HEAD, 8, HD), bf16),
        ((2 * TOK + N_SEQ * TAIL, HD), bf16),
        ((2 * KEYS + N_SEQ * TAIL, HD), f32),
        ((3 * TOK, HD), f32),
    ]
    return pl.pallas_call(
        project_kernel,
        name="project",
        out_shape=tuple(jax.ShapeDtypeStruct(shape, dtype) for shape, dtype in outputs),
        in_specs=[hbm] * 10 + [smem],
        out_specs=(hbm,) * 4,
        scratch_shapes=[pltpu.VMEM(shape, dtype) for shape, dtype in outputs]
        + [
            pltpu.VMEM((ROWS, width), bf16),
            pltpu.VMEM((width, 2 * HD), bf16),
            pltpu.VMEM((64, width), bf16),
            pltpu.VMEM((width,), bf16),
            pltpu.VMEM((2 * HD,), bf16),
            pltpu.VMEM((4, 8), bf16),
            pltpu.VMEM((1, IMG), jnp.int32),
            pltpu.VMEM((1, HD), f32),
            pltpu.VMEM((2, ROWS, HD), f32),
            pltpu.SemaphoreType.DMA((4 + KCH,)),
            pltpu.SemaphoreType.DMA((5,)),
            pltpu.SemaphoreType.DMA((4,)),
        ],
        compiler_params=pltpu.CompilerParams(vmem_limit_bytes=LIMIT),
    )


def panel_call():
    return pl.pallas_call(
        panel_kernel,
        name="panel",
        out_shape=jax.ShapeDtypeStruct((N_SEQ, PAY, HD), bf16),
        in_specs=[vmem()] * 3,
        out_specs=vmem(),
        compiler_params=small_params(),
    )


def body(
    embedded,
    norm_gain,
    query_weight,
    query_bias,
    key_weight,
    value_weight,
    value_bias,
    image_rows,
    image_dest,
    doc_lengths,
    block_mask,
):
    width = embedded.shape[1]
    half = np.arange(HD) % (HD // 2)
    inverse = jnp.asarray((rope_base ** (-2.0 * half / HD)).astype(np.float32)[None, :])
    smem = pl.BlockSpec(memory_space=pltpu.SMEM)
    key_t = jnp.transpose(key_weight, (1, 2, 0)).reshape(32, width)
    value_t = jnp.transpose(value_weight, (1, 2, 0)).reshape(32, width)
    kv_send, share, aux, own = project_call(width)(
        embedded, image_rows, query_weight, key_t, value_t, norm_gain, query_bias,
        value_bias, image_dest[None, :], inverse, doc_lengths,
    )
    chip_swap = [(i, i ^ 2) for i in range(N_HEAD)]
    core_swap = [(i, i ^ 1) for i in range(N_HEAD)]
    shared = lax.ppermute(share, "head", chip_swap)
    kv_mine = lax.all_to_all(kv_send, "head", 0, 0)
    payload = panel_call()(kv_mine, aux, shared)
    mine = lax.all_to_all(payload, "seq", 0, 0)
    other = lax.ppermute(mine, "head", core_swap)
    merged, where, start = pl.pallas_call(
        place_kernel,
        name="place",
        out_shape=(
            jax.ShapeDtypeStruct((4 * TOK, HD), bf16),
            jax.ShapeDtypeStruct((TILES, HD), f32),
            jax.ShapeDtypeStruct((TOK, HD), f32),
        ),
        in_specs=[vmem()] * 3 + [smem],
        out_specs=(vmem(),) * 3,
        compiler_params=small_params(),
        cost_estimate=pl.CostEstimate(flops=1 << 28, bytes_accessed=1 << 20, transcendentals=0),
    )(own, shared, mine, block_mask)
    keep, send = pl.pallas_call(
        attend_kernel,
        name="attend",
        out_shape=(
            jax.ShapeDtypeStruct((3, 2 * TOK, HD), f32),
            jax.ShapeDtypeStruct((2 * TOK + 16, HD), bf16),
        ),
        in_specs=[vmem()] * 5,
        out_specs=(vmem(), vmem()),
        scratch_shapes=[pltpu.VMEM((TILES, 4 * TOK, HD), f32)],
        compiler_params=small_params(),
    )(merged, where, start, mine, other)
    come = lax.ppermute(send, "head", chip_swap)
    return pl.pallas_call(
        combine_kernel,
        name="combine",
        out_shape=jax.ShapeDtypeStruct((TOK, 2 * HD), bf16),
        in_specs=[vmem()] * 2,
        out_specs=vmem(),
        compiler_params=small_params(),
    )(keep, come)


def solution(mesh):
    in_specs = (
        P("seq", None),
        P(),
        P(None, "head"),
        P("head"),
        P(None, None, "head"),
        P(None, None, "head"),
        P(None, "head"),
        P("seq", None),
        P("seq"),
        P(),
        P("seq", None),
    )
    out_specs = P("seq", "head")
    return jax.shard_map(body, mesh=mesh, in_specs=in_specs, out_specs=out_specs, check_vma=False)
```

time: 63.9 us -> 61.2 us (0.958)
  blocking collectives: 46.7 us -> 39 us
  waiting for transfers between devices: 0.01 us -> 3.53 us
  starting transfers between devices: 2.05 us -> 5.13 us
  local copies, waits for them, and re-layouts: 3.44 us -> 1.87 us
    all_to_all x1, blocking collectives: 34 us -> 27.1 us  [body(): mine = lax.all_to_all(payload, 'seq', 0, 0)]
    ppermute x1 -> x3, waiting for transfers between devices: 0.01 us -> 3.53 us  [the longest x1 3.53 us: body(): come = lax.ppermute(send, 'head', chip_swap)]
    ppermute x1 -> x3, starting transfers between devices: 2.05 us -> 5.13 us  [the longest x1 2.54 us: body(): other = lax.ppermute(mine, 'head', core_swap)]
    unnamed x10 -> x6, local copies, waits for them, and re-layouts: 3.44 us -> 1.87 us
    all_to_all x1, blocking collectives: 12.7 us -> 11.9 us  [body(): kv_mine = lax.all_to_all(kv_send, 'head', 0, 0)]
    pallas_call x2 -> x3, Pallas kernels: 3.19 us -> 3.17 us  [the longest x1 2.22 us: body(): pl.pallas_call(attend_kernel, name='attend', out_shape=(jax.ShapeDtypeStr...]
  transfers between devices with their start and end apart: 1 -> 3, of which waited for: 0 -> 1; matrix products, arithmetic and copies ran while one was open for 0% -> 0% of each run, Pallas kernels for 2% -> 2%
where the time goes in v3:
time: 61.2 us; the launch traced here: 61 us
  blocking collectives  39 us (64%)
  Pallas kernels  11.4 us (19%)
  starting transfers between devices  5.13 us (8%)
  waiting for transfers between devices  3.53 us (6%)
  local copies, waits for them, and re-layouts  1.87 us (3%)
    all_to_all x1, blocking collectives, body(): mine = lax.all_to_all(payload, 'seq', 0, 0)  27.1 us
    all_to_all x1, blocking collectives, body(): kv_mine = lax.all_to_all(kv_send, 'head', 0, 0)  11.9 us
    pallas_call x1, Pallas kernels, body(): project_call(width)  7.02 us
    ppermute x1, waiting for transfers between devices, body(): come = lax.ppermute(send, 'head', chip_swap)  3.53 us
    ppermute x1, starting transfers between devices, body(): other = lax.ppermute(mine, 'head', core_swap)  2.54 us
    pallas_call x1, Pallas kernels, body(): pl.pallas_call(attend_kernel, name='attend', out_shape=(jax.ShapeDtypeStr...  2.22 us
    ppermute x1, starting transfers between devices, body(): shared = lax.ppermute(share, 'head', chip_swap)  2.22 us
    unnamed x6, local copies, waits for them, and re-layouts  1.87 us
  transfers between devices with their start and end apart: 3, of which 1 were waited for; matrix products, arithmetic and copies ran while one was open for 0% of the time, Pallas kernels for 2%

profile of v3, /device:TPU:1, one launch (start us, length us, event | category | flops | bytes accessed | tf_op | source)
XLA Modules:
  0.0 61.0 jit_solution(11038334874210502313)
XLA Ops:
  0.0 0.0 copy-start.2
  0.0 7.0 %project.1 = (bf16[16,8,128]{2,1,0:T(8,128)(2,1)}, bf16[512,128]{1,0:T(8,128)(2,1)}, f32[432,128]{1,0:T(8,128)}, f32[384,128]{1,0:T(8,128)}) custom-call(bf16[128,8192]{1,0:T(8,128)(2,1)} %x_hbm.1, bf16[48,8192]{1,0:T(8,128)(2,1)} %img_hbm.1, bf16[8192,256]{1,0:T(8,128)(2,1)} %wq_hbm.1, bf16[32,8192]{1,0:T(8,128)(2,1)} %bitcast.7, bf16[32,8192]{1,0:T(8,128)(2,1)} %bitcast.8, ...), custom_call_target="tpu_custom_call" | custom-call | tf_op jit(solution)/shard_map/project/pallas_call | solution.py:431
  7.0 2.2 %collective-permute-start = (bf16[512,128]{1,0:T(8,128)(2,1)}, bf16[512,128]{1,0:T(8,128)(2,1)S(1)}, u32[]{:S(2)}, u32[]{:S(2)}) collective-permute-start(bf16[512,128]{1,0:T(8,128)(2,1)} %get-tuple-element.15), channel_id=1, source_target_pairs={{0,2},{1,3},{2,0},{3,1},{4,6},{5,7},{6,4},{7,5},{8,10},{9,11},{10,... | collective-permute-start | bytes 393224 | tf_op jit(solution)/shard_map/ppermute | solution.py:437
  9.2 11.9 %all_to_all.10.kv_ref = bf16[16,8,128]{2,1,0:T(8,128)(2,1)S(1)} all-to-all(bf16[16,8,128]{2,1,0:T(8,128)(2,1)} %get-tuple-element.16), channel_id=1, replica_groups=mesh['seq'=16,'head'=16] {'head'}, dimensions={0} | all-to-all | bytes 65536 | tf_op jit(solution)/shard_map/all_to_all | solution.py:438
  21.1 0.0 collective-permute-done.share_ref
  21.1 0.0 copy-start
  21.1 0.9 %copy-done = f32[432,128]{1,0:T(8,128)S(1)} copy-done((f32[432,128]{1,0:T(8,128)S(1)}, f32[432,128]{1,0:T(8,128)}, u32[]{:S(2)}) %copy-start) | copy-done | bytes 221208
  22.1 0.2 panel.1
  22.2 27.1 %all_to_all.11.mine_ref = bf16[16,120,128]{2,1,0:T(8,128)(2,1)S(1)} all-to-all(bf16[16,120,128]{2,1,0:T(8,128)(2,1)S(1)} %panel.1), channel_id=1, replica_groups=mesh['seq'=16,'head'=16] {'seq'}, dimensions={0} | all-to-all | bytes 983040 | tf_op jit(solution)/shard_map/all_to_all | solution.py:440
  49.3 2.5 %collective-permute-start.1 = (bf16[16,120,128]{2,1,0:T(8,128)(2,1)S(1)}, bf16[16,120,128]{2,1,0:T(8,128)(2,1)S(1)}, u32[]{:S(2)}, u32[]{:S(2)}) collective-permute-start(bf16[16,120,128]{2,1,0:T(8,128)(2,1)S(1)} %all_to_all.11.mine_ref), channel_id=1, source_target_pairs={{0,1},{1,0},{2,3},{3,2},{4,5},{5,4},{6,7},{7,6},{8,9},{9,8},{10,11... | collective-permute-start | bytes 1474568 | tf_op jit(solution)/shard_map/ppermute | solution.py:441
  51.9 0.0 copy-done.2
  51.9 0.0 copy-start.1
  51.9 0.9 %copy-done.1 = f32[384,128]{1,0:T(8,128)S(1)} copy-done((f32[384,128]{1,0:T(8,128)S(1)}, f32[384,128]{1,0:T(8,128)}, u32[]{:S(2)}) %copy-start.1) | copy-done | bytes 196632
  52.8 1.3 %place.1 = (bf16[512,128]{1,0:T(8,128)(2,1)S(1)}, f32[12,128]{1,0:T(8,128)S(1)}, f32[128,128]{1,0:T(8,128)S(1)}) custom-call(f32[384,128]{1,0:T(8,128)S(1)} %copy-done.1, bf16[512,128]{1,0:T(8,128)(2,1)S(1)} %collective-permute-done.share_ref, bf16[16,120,128]{2,1,0:T(8,128)(2,1)S(1)} %all_to_all.11.mine_ref, s32[1,16]{1,0:T(1,128)S(1)} %copy-done.2), custom_call_target="tpu_custom_call" | custom-call | flops 268435456 | bytes 1048576 | tf_op jit(solution)/shard_map/place/pallas_call | solution.py:442
  54.1 0.0 collective-permute-done.1.other_ref
  54.1 2.2 %attend.1 = (f32[3,256,128]{2,1,0:T(8,128)S(1)}, bf16[272,128]{1,0:T(8,128)(2,1)S(1)}) custom-call(bf16[512,128]{1,0:T(8,128)(2,1)S(1)} %get-tuple-element.18.q_ref, f32[12,128]{1,0:T(8,128)S(1)} %get-tuple-element.19.where_ref, f32[128,128]{1,0:T(8,128)S(1)} %get-tuple-element.20.start_ref, bf16[16,120,128]{2,1,0:T(8,128)(2,1)S(1)} %all_to_all.11.mine_ref, ...), custom_call_target="tpu_custom_call" | custom-call | tf_op jit(solution)/shard_map/attend/pallas_call | solution.py:455
  56.3 0.4 collective-permute-start.2
  56.7 3.5 %collective-permute-done.2.come_ref = bf16[272,128]{1,0:T(8,128)(2,1)S(1)} collective-permute-done((bf16[272,128]{1,0:T(8,128)(2,1)S(1)}, bf16[272,128]{1,0:T(8,128)(2,1)S(1)}, u32[]{:S(2)}, u32[]{:S(2)}) %collective-permute-start.2) | collective-permute-done | bytes 69664 | tf_op jit(solution)/shard_map/ppermute | solution.py:467
  60.2 0.8 %combine.1 = bf16[128,256]{1,0:T(8,128)(2,1)} custom-call(f32[3,256,128]{2,1,0:T(8,128)S(1)} %get-tuple-element.21.keep_ref, bf16[272,128]{1,0:T(8,128)(2,1)S(1)} %collective-permute-done.2.come_ref), custom_call_target="tpu_custom_call" | custom-call | tf_op jit(solution)/shard_map/combine/pallas_call | solution.py:468
Async XLA Ops:
  0.0 51.9 %copy-start.2 = (s32[1,16]{1,0:T(1,128)S(1)}, s32[1,16]{1,0:T(1,128)}, u32[]{:S(2)}) copy-start(s32[1,16]{1,0:T(1,128)} %mask_ref.1) | copy-start | bytes 196
  7.0 14.1 %collective-permute-start = (bf16[512,128]{1,0:T(8,128)(2,1)}, bf16[512,128]{1,0:T(8,128)(2,1)S(1)}, u32[]{:S(2)}, u32[]{:S(2)}) collective-permute-start(bf16[512,128]{1,0:T(8,128)(2,1)} %get-tuple-element.15), channel_id=1, source_target_pairs={{0,2},{1,3},{2,0},{3,1},{4,6},{5,7},{6,4},{7,5},{8,10},{9,11},{10,... | collective-permute-start | bytes 393224 | tf_op jit(solution)/shard_map/ppermute | solution.py:437
  21.1 0.9 %copy-start = (f32[432,128]{1,0:T(8,128)S(1)}, f32[432,128]{1,0:T(8,128)}, u32[]{:S(2)}) copy-start(f32[432,128]{1,0:T(8,128)} %get-tuple-element.17.aux_ref) | copy-start | bytes 663556
  49.3 4.7 %collective-permute-start.1 = (bf16[16,120,128]{2,1,0:T(8,128)(2,1)S(1)}, bf16[16,120,128]{2,1,0:T(8,128)(2,1)S(1)}, u32[]{:S(2)}, u32[]{:S(2)}) collective-permute-start(bf16[16,120,128]{2,1,0:T(8,128)(2,1)S(1)} %all_to_all.11.mine_ref), channel_id=1, source_target_pairs={{0,1},{1,0},{2,3},{3,2},{4,5},{5,4},{6,7},{7,6},{8,9},{9,8},{10,11... | collective-permute-start | bytes 1474568 | tf_op jit(solution)/shard_map/ppermute | solution.py:441
  51.9 0.9 %copy-start.1 = (f32[384,128]{1,0:T(8,128)S(1)}, f32[384,128]{1,0:T(8,128)}, u32[]{:S(2)}) copy-start(f32[384,128]{1,0:T(8,128)} %get-tuple-element.14.own_ref) | copy-start | bytes 589828
  56.3 3.9 %collective-permute-start.2 = (bf16[272,128]{1,0:T(8,128)(2,1)S(1)}, bf16[272,128]{1,0:T(8,128)(2,1)S(1)}, u32[]{:S(2)}, u32[]{:S(2)}) collective-permute-start(bf16[272,128]{1,0:T(8,128)(2,1)S(1)} %get-tuple-element.22), channel_id=1, source_target_pairs={{0,2},{1,3},{2,0},{3,1},{4,6},{5,7},{6,4},{7,5},{8,10},{9,11},{10,... | collective-permute-start | bytes 208904 | tf_op jit(solution)/shard_map/ppermute | solution.py:467

commit v4 on v3

--- a/solution.py
+++ b/solution.py
@@ -56,9 +56,9 @@
 
 
 def project_kernel(
-    x_hbm, img_hbm, wq_hbm, wk_hbm, wv_hbm, gain_hbm, bq_hbm, bv_hbm, dest_hbm, invf_hbm, docs_ref,
-    kv_hbm, share_hbm, aux_hbm, own_hbm,
-    kv_ref, share, aux, own, xs, wqs, wkvs, gains, bqs, bvs, dests, invfs, css, sems, small_sems, out_sems,
+    x_hbm, img_hbm, wq_hbm, wk_hbm, wv_hbm, gain_hbm, bq_hbm, bv_hbm, dest_hbm, invf_hbm, docs_hbm,
+    kv_ref, share, aux, own,
+    xs, wqs, wkvs, gains, bqs, bvs, dests, invfs, docs_ref, css, sems, small_sems,
 ):
     width = xs.shape[1]
     step = width // KCH
@@ -74,13 +74,25 @@
     small = [
         pltpu.make_async_copy(src, dst, small_sems.at[i])
         for i, (src, dst) in enumerate(
-            ((dest_hbm, dests), (invf_hbm, invfs), (gain_hbm, gains), (bq_hbm, bqs), (bv_hbm, bvs))
+            ((docs_hbm, docs_ref), (dest_hbm, dests), (invf_hbm, invfs), (gain_hbm, gains), (bq_hbm, bqs), (bv_hbm, bvs))
         )
     ]
-    for copy in small[:2] + copies[:2] + small[2:] + copies[2:]:
+    for copy in small[:3] + copies[:2] + small[3:] + copies[2:]:
         copy.start()
-    small[0].wait()
-    small[1].wait()
+    inverse = []
+    for i, rows in enumerate((pl.ds(0, TOK), pl.ds(TOK, IMG))):
+        copies[i].wait()
+        squares = jnp.zeros((rows.size, HD), f32)
+        for c in range(width // HD):
+            wide = xs[rows, c * HD : (c + 1) * HD].astype(f32)
+            squares = squares + wide * wide
+        inverse.append(
+            lax.rsqrt(jnp.sum(squares, axis=1, keepdims=True) * (1.0 / width) + norm_eps)
+        )
+    inverse = jnp.concatenate(inverse, axis=0)
+
+    for copy in small[:3]:
+        copy.wait()
 
     seq_place = lax.axis_index("seq")
     first = (seq_place * TOK).astype(f32)
@@ -134,32 +146,14 @@
     wide_slot = iota((count, HD), 0) % TAIL
     tail = tail + jnp.where(wide_slot == 12, hi_two, jnp.where(wide_slot == 13, lo_two, 0.0))
 
-    outs = [
-        pltpu.make_async_copy(kv_ref, kv_hbm, out_sems.at[0]),
-        pltpu.make_async_copy(share, share_hbm, out_sems.at[1]),
-        pltpu.make_async_copy(own, own_hbm, out_sems.at[2]),
-        pltpu.make_async_copy(aux, aux_hbm, out_sems.at[3]),
-    ]
-
-    inverse = []
-    for i, rows in enumerate((pl.ds(0, TOK), pl.ds(TOK, IMG))):
-        copies[i].wait()
-        squares = jnp.zeros((rows.size, HD), f32)
-        for c in range(width // HD):
-            wide = xs[rows, c * HD : (c + 1) * HD].astype(f32)
-            squares = squares + wide * wide
-        inverse.append(
-            lax.rsqrt(jnp.sum(squares, axis=1, keepdims=True) * (1.0 / width) + norm_eps)
-        )
-    inverse = jnp.concatenate(inverse, axis=0)
-
-    for copy in small[2:] + copies[2:4]:
+    for copy in small[3:] + copies[2:4]:
         copy.wait()
     queries = jnp.broadcast_to(bqs[...].astype(f32).reshape(1, 2 * HD), (ROWS, 2 * HD))
     kv = jnp.zeros((ROWS, 64), f32)
-    for copy in copies[4:]:
-        copy.wait()
     for c in range(KCH):
+        if c % 2 == 0:
+            copies[4 + c].wait()
+            copies[5 + c].wait()
         part = pl.ds(c * step, step)
         gain = gains[part].astype(f32).reshape(1, step)
         normed = (xs[:, part].astype(f32) * inverse * gain).astype(bf16)
@@ -184,7 +178,6 @@
             bias = jnp.sum(jnp.where(eye8, bias_row, 0.0), axis=1, keepdims=True)
             kv_ref[4 * g + 2 * j] = kv_t[8 * g : 8 * g + 8].astype(bf16)
             kv_ref[4 * g + 2 * j + 1] = (kv_t[32 + 8 * g : 40 + 8 * g] + bias).astype(bf16)
-    outs[0].start()
 
     cosine = css[0]
     sine = css[1]
@@ -197,13 +190,8 @@
         tail = tail + jnp.dot(
             jnp.where(pick, 1.0, 0.0).astype(bf16), v[TOK:], preferred_element_type=f32
         )
-    outs[2].start()
     share[2 * TOK :, :] = tail.astype(bf16)
-    outs[1].start()
     aux[2 * KEYS :, :] = tail
-    outs[3].start()
-    for out in outs:
-        out.wait()
 
 
 def panel_kernel(kv_ref, aux_ref, share_ref, pay_ref):
@@ -280,7 +268,9 @@
         where_ref[m : m + 1, :] = jnp.where((taken < 0.5) & (seen == 1), position, BIG)
 
 
-def attend_kernel(q_ref, where_ref, start_ref, mine_ref, other_ref, keep_ref, send_ref, scores):
+def attend_kernel(far, q_ref, where_ref, start_ref, mine_ref, other_ref, *rest):
+    scores = rest[-1]
+    count = 2 * TOK
     is_key = lax.axis_index("head") % 2 == 0
     first = (lax.axis_index("seq") * TOK).astype(f32)
     slope = math.log2(math.e) / math.sqrt(HD)
@@ -292,32 +282,35 @@
         return ref[4 * m : 4 * m + 4, HALF_TOK : HALF_TOK + 32, :].reshape(HD, HD)
 
     def attend(keys, values):
-        queries = q_ref[...]
+        queries = q_ref[count:, :] if far else q_ref[:count, :]
         position = first + fiota((TOK, HD), 0)
         start = start_ref[...]
-        top = jnp.full((4 * TOK, HD), NEG, f32)
+        top = jnp.full((count, HD), NEG, f32)
         for t in range(TILES):
             where = where_ref[t : t + 1, :]
             allowed = (where <= position) & (where >= start)
-            allowed = jnp.concatenate([allowed] * 4, axis=0)
+            allowed = jnp.concatenate([allowed] * 2, axis=0)
             score = jnp.where(allowed, dot_t(queries, tile_of(keys, t)), NEG)
             scores[t] = score
             top = jnp.maximum(top, score)
         top = jnp.maximum(jnp.max(top, axis=1, keepdims=True), LOW)
-        total = jnp.zeros((4 * TOK, HD), f32)
-        mix = jnp.zeros((4 * TOK, HD), f32)
+        total = jnp.zeros((count, HD), f32)
+        mix = jnp.zeros((count, HD), f32)
         for t in range(TILES):
             weight = jnp.exp2((scores[t] - top) * slope)
             total = total + weight
             mix = mix + jnp.dot(weight.astype(bf16), tile_of(values, t), preferred_element_type=f32)
         total = jnp.sum(total, axis=1, keepdims=True)
-        mine = 2 * TOK
-        keep_ref[0] = mix[:mine]
-        keep_ref[1] = jnp.broadcast_to(top[:mine], (mine, HD))
-        keep_ref[2] = jnp.broadcast_to(total[:mine], (mine, HD))
-        send_ref[0:mine, :] = (mix[mine:] / jnp.maximum(total[mine:], 1.0e-30)).astype(bf16)
+        if not far:
+            keep_ref = rest[0]
+            keep_ref[0] = mix
+            keep_ref[1] = jnp.broadcast_to(top, (count, HD))
+            keep_ref[2] = jnp.broadcast_to(total, (count, HD))
+            return
+        send_ref = rest[0]
+        send_ref[0:count, :] = (mix / jnp.maximum(total, 1.0e-30)).astype(bf16)
         rows = []
-        for column in (top[mine:], total[mine:]):
+        for column in (top, total):
             for e in range(2):
                 part = jnp.broadcast_to(column[e * TOK : (e + 1) * TOK], (TOK, HD))
                 left = jnp.transpose(part)[0:1]
@@ -326,7 +319,7 @@
                     rows.append(piece)
                     left = left - piece
         rows.append(jnp.zeros((4, HD), f32))
-        send_ref[mine:, :] = jnp.concatenate(rows, axis=0).astype(bf16)
+        send_ref[count:, :] = jnp.concatenate(rows, axis=0).astype(bf16)
 
     @pl.when(is_key)
     def _():
@@ -366,21 +359,19 @@
 
 def project_call(width):
     hbm = pl.BlockSpec(memory_space=pltpu.HBM)
-    smem = pl.BlockSpec(memory_space=pltpu.SMEM)
     outputs = [
         ((N_HEAD, 8, HD), bf16),
         ((2 * TOK + N_SEQ * TAIL, HD), bf16),
         ((2 * KEYS + N_SEQ * TAIL, HD), f32),
         ((3 * TOK, HD), f32),
     ]
-    return pl.pallas_call(
+    call = pl.pallas_call(
         project_kernel,
         name="project",
         out_shape=tuple(jax.ShapeDtypeStruct(shape, dtype) for shape, dtype in outputs),
-        in_specs=[hbm] * 10 + [smem],
-        out_specs=(hbm,) * 4,
-        scratch_shapes=[pltpu.VMEM(shape, dtype) for shape, dtype in outputs]
-        + [
+        in_specs=[hbm] * 11,
+        out_specs=(vmem(),) * 4,
+        scratch_shapes=[
             pltpu.VMEM((ROWS, width), bf16),
             pltpu.VMEM((width, 2 * HD), bf16),
             pltpu.VMEM((64, width), bf16),
@@ -389,12 +380,29 @@
             pltpu.VMEM((4, 8), bf16),
             pltpu.VMEM((1, IMG), jnp.int32),
             pltpu.VMEM((1, HD), f32),
+            pltpu.SMEM((DOCS,), jnp.int32),
             pltpu.VMEM((2, ROWS, HD), f32),
             pltpu.SemaphoreType.DMA((4 + KCH,)),
-            pltpu.SemaphoreType.DMA((5,)),
-            pltpu.SemaphoreType.DMA((4,)),
+            pltpu.SemaphoreType.DMA((6,)),
         ],
-        compiler_params=pltpu.CompilerParams(vmem_limit_bytes=LIMIT),
+        compiler_params=pltpu.CompilerParams(vmem_limit_bytes=20 << 20),
+    )
+    return lambda *arrays: call(
+        *(pltpu.with_memory_space_constraint(array, pltpu.HBM) for array in arrays)
+    )
+
+
+def attend_call(far):
+    out = ((2 * TOK + 16, HD), bf16) if far else ((3, 2 * TOK, HD), f32)
+    return pl.pallas_call(
+        functools.partial(attend_kernel, far),
+        name="attend_far" if far else "attend_near",
+        out_shape=jax.ShapeDtypeStruct(*out),
+        in_specs=[vmem()] * 5,
+        out_specs=vmem(),
+        scratch_shapes=[pltpu.VMEM((TILES, 2 * TOK, HD), f32)],
+        compiler_params=small_params(),
+        cost_estimate=pl.CostEstimate(flops=1 << 30, bytes_accessed=1 << 21, transcendentals=1 << 19),
     )
 
 
@@ -452,19 +460,9 @@
         compiler_params=small_params(),
         cost_estimate=pl.CostEstimate(flops=1 << 28, bytes_accessed=1 << 20, transcendentals=0),
     )(own, shared, mine, block_mask)
-    keep, send = pl.pallas_call(
-        attend_kernel,
-        name="attend",
-        out_shape=(
-            jax.ShapeDtypeStruct((3, 2 * TOK, HD), f32),
-            jax.ShapeDtypeStruct((2 * TOK + 16, HD), bf16),
-        ),
-        in_specs=[vmem()] * 5,
-        out_specs=(vmem(), vmem()),
-        scratch_shapes=[pltpu.VMEM((TILES, 4 * TOK, HD), f32)],
-        compiler_params=small_params(),
-    )(merged, where, start, mine, other)
+    send = attend_call(True)(merged, where, start, mine, other)
     come = lax.ppermute(send, "head", chip_swap)
+    keep = attend_call(False)(merged, where, start, mine, other)
     return pl.pallas_call(
         combine_kernel,
         name="combine",

time: 61.2 us -> 55.9 us (0.913)
  local copies, waits for them, and re-layouts: 1.87 us -> 0.01 us
  waiting for transfers between devices: 3.53 us -> 1.81 us
  Pallas kernels: 11.4 us -> 9.99 us
    ppermute x1, waiting for transfers between devices: 3.53 us -> 1.58 us  [body(): come = lax.ppermute(send, 'head', chip_swap)]
    unnamed x6 -> x2, local copies, waits for them, and re-layouts: 1.87 us -> 0.01 us
    pallas_call x2 -> x3, Pallas kernels: 9.24 us -> 7.78 us  [the longest x1 5.24 us: project_call(): call(*(pltpu.with_memory_space_constraint(array, pltpu.HBM) for array in...]
  transfers between devices with their start and end apart: 3 -> 3, of which waited for: 1 -> 2; matrix products, arithmetic and copies ran while one was open for 0% -> 0% of each run, Pallas kernels for 2% -> 5%
where the time goes in v4:
time: 55.9 us; the launch traced here: 55.7 us
  blocking collectives  38.7 us (69%)
  Pallas kernels  9.99 us (18%)
  starting transfers between devices  5.13 us (9%)
  waiting for transfers between devices  1.81 us (3%)
    all_to_all x1, blocking collectives, body(): mine = lax.all_to_all(payload, 'seq', 0, 0)  27.1 us
    all_to_all x1, blocking collectives, body(): kv_mine = lax.all_to_all(kv_send, 'head', 0, 0)  11.7 us
    pallas_call x1, Pallas kernels, project_call(): call(*(pltpu.with_memory_space_constraint(array, pltpu.HBM) for array in...  5.24 us
    ppermute x1, starting transfers between devices, body(): other = lax.ppermute(mine, 'head', core_swap)  2.54 us
    ppermute x1, starting transfers between devices, body(): shared = lax.ppermute(share, 'head', chip_swap)  2.21 us
    ppermute x1, waiting for transfers between devices, body(): come = lax.ppermute(send, 'head', chip_swap)  1.58 us
    pallas_call x1, Pallas kernels, body(): keep = attend_call(False)(merged, where, start, mine, other)  1.29 us
    pallas_call x1, Pallas kernels, body(): pl.pallas_call(place_kernel, name='place', out_shape=(jax.ShapeDtypeStruc...  1.26 us
  transfers between devices with their start and end apart: 3, of which 2 were waited for; matrix products, arithmetic and copies ran while one was open for 0% of the time, Pallas kernels for 5%

profile of v4, /device:TPU:1, one launch (start us, length us, event | category | flops | bytes accessed | tf_op | source)
XLA Modules:
  0.0 55.7 jit_solution(16421355424135879239)
XLA Ops:
  0.0 0.0 copy-start
  0.0 5.2 %project.1 = (bf16[16,8,128]{2,1,0:T(8,128)(2,1)S(1)}, bf16[512,128]{1,0:T(8,128)(2,1)S(1)}, f32[432,128]{1,0:T(8,128)S(1)}, f32[384,128]{1,0:T(8,128)S(1)}) custom-call(bf16[128,8192]{1,0:T(8,128)(2,1)} %x_hbm.1, bf16[48,8192]{1,0:T(8,128)(2,1)} %img_hbm.1, bf16[8192,256]{1,0:T(8,128)(2,1)} %wq_hbm.1, bf16[32,8192]{1,0:T(8,128)(2,1)} %bitcast.7, ...), custom_call_target="tpu_custom_call" | custom-call | tf_op jit(solution)/shard_map/project/pallas_call | solution.py:390
  5.3 2.2 %collective-permute-start = (bf16[512,128]{1,0:T(8,128)(2,1)S(1)}, bf16[512,128]{1,0:T(8,128)(2,1)S(1)}, u32[]{:S(2)}, u32[]{:S(2)}) collective-permute-start(bf16[512,128]{1,0:T(8,128)(2,1)S(1)} %get-tuple-element.13), channel_id=1, source_target_pairs={{0,2},{1,3},{2,0},{3,1},{4,6},{5,7},{6,4},{7,5},{8,10},{9,11},{10,... | collective-permute-start | bytes 393224 | tf_op jit(solution)/shard_map/ppermute | solution.py:445
  7.5 11.7 %all_to_all.10.kv_ref = bf16[16,8,128]{2,1,0:T(8,128)(2,1)S(1)} all-to-all(bf16[16,8,128]{2,1,0:T(8,128)(2,1)S(1)} %get-tuple-element.14), channel_id=1, replica_groups=mesh['seq'=16,'head'=16] {'head'}, dimensions={0} | all-to-all | bytes 65536 | tf_op jit(solution)/shard_map/all_to_all | solution.py:446
  19.1 0.0 collective-permute-done.share_ref
  19.1 0.2 panel.1
  19.3 27.1 %all_to_all.11.mine_ref = bf16[16,120,128]{2,1,0:T(8,128)(2,1)S(1)} all-to-all(bf16[16,120,128]{2,1,0:T(8,128)(2,1)S(1)} %panel.1), channel_id=1, replica_groups=mesh['seq'=16,'head'=16] {'seq'}, dimensions={0} | all-to-all | bytes 983040 | tf_op jit(solution)/shard_map/all_to_all | solution.py:448
  46.4 2.5 %collective-permute-start.1 = (bf16[16,120,128]{2,1,0:T(8,128)(2,1)S(1)}, bf16[16,120,128]{2,1,0:T(8,128)(2,1)S(1)}, u32[]{:S(2)}, u32[]{:S(2)}) collective-permute-start(bf16[16,120,128]{2,1,0:T(8,128)(2,1)S(1)} %all_to_all.11.mine_ref), channel_id=1, source_target_pairs={{0,1},{1,0},{2,3},{3,2},{4,5},{5,4},{6,7},{7,6},{8,9},{9,8},{10,11... | collective-permute-start | bytes 1474568 | tf_op jit(solution)/shard_map/ppermute | solution.py:449
  48.9 0.0 copy-done
  48.9 1.3 %place.1 = (bf16[512,128]{1,0:T(8,128)(2,1)S(1)}, f32[12,128]{1,0:T(8,128)S(1)}, f32[128,128]{1,0:T(8,128)S(1)}) custom-call(f32[384,128]{1,0:T(8,128)S(1)} %get-tuple-element.12.own_ref, bf16[512,128]{1,0:T(8,128)(2,1)S(1)} %collective-permute-done.share_ref, bf16[16,120,128]{2,1,0:T(8,128)(2,1)S(1)} %all_to_all.11.mine_ref, s32[1,16]{1,0:T(1,128)S(1)} %copy-done), custom_call_target="tpu_custom_call" | custom-call | flops 268435456 | bytes 1048576 | tf_op jit(solution)/shard_map/place/pallas_call | solution.py:450
  50.2 0.2 collective-permute-done.1.other_ref
  50.4 1.2 %attend_far.1 = bf16[272,128]{1,0:T(8,128)(2,1)S(1)} custom-call(bf16[512,128]{1,0:T(8,128)(2,1)S(1)} %get-tuple-element.16.q_ref, f32[12,128]{1,0:T(8,128)S(1)} %get-tuple-element.17.where_ref, f32[128,128]{1,0:T(8,128)S(1)} %get-tuple-element.18.start_ref, bf16[16,120,128]{2,1,0:T(8,128)(2,1)S(1)} %all_to_all.11.mine_ref, ...), custom_call_target="tpu_custom_call" | custom-call | flops 1073741824 | bytes 2097152 | tf_op jit(solution)/shard_map/attend_far/pallas_call | solution.py:463
  51.7 0.4 collective-permute-start.2
  52.1 1.3 %attend_near.1.keep_ref = f32[3,256,128]{2,1,0:T(8,128)S(1)} custom-call(bf16[512,128]{1,0:T(8,128)(2,1)S(1)} %get-tuple-element.16.q_ref, f32[12,128]{1,0:T(8,128)S(1)} %get-tuple-element.17.where_ref, f32[128,128]{1,0:T(8,128)S(1)} %get-tuple-element.18.start_ref, bf16[16,120,128]{2,1,0:T(8,128)(2,1)S(1)} %all_to_all.11.mine_ref, ...), custom_call_target="tpu_custom_call" | custom-call | flops 1073741824 | bytes 2097152 | tf_op jit(solution)/shard_map/attend_near/pallas_call | solution.py:465
  53.3 1.6 %collective-permute-done.2.come_ref = bf16[272,128]{1,0:T(8,128)(2,1)S(1)} collective-permute-done((bf16[272,128]{1,0:T(8,128)(2,1)S(1)}, bf16[272,128]{1,0:T(8,128)(2,1)S(1)}, u32[]{:S(2)}, u32[]{:S(2)}) %collective-permute-start.2) | collective-permute-done | bytes 69664 | tf_op jit(solution)/shard_map/ppermute | solution.py:464
  54.9 0.8 %combine.1 = bf16[128,256]{1,0:T(8,128)(2,1)} custom-call(f32[3,256,128]{2,1,0:T(8,128)S(1)} %attend_near.1.keep_ref, bf16[272,128]{1,0:T(8,128)(2,1)S(1)} %collective-permute-done.2.come_ref), custom_call_target="tpu_custom_call" | custom-call | tf_op jit(solution)/shard_map/combine/pallas_call | solution.py:466
Async XLA Ops:
  0.0 48.9 %copy-start = (s32[1,16]{1,0:T(1,128)S(1)}, s32[1,16]{1,0:T(1,128)}, u32[]{:S(2)}) copy-start(s32[1,16]{1,0:T(1,128)} %mask_ref.1) | copy-start | bytes 196
  5.3 13.9 %collective-permute-start = (bf16[512,128]{1,0:T(8,128)(2,1)S(1)}, bf16[512,128]{1,0:T(8,128)(2,1)S(1)}, u32[]{:S(2)}, u32[]{:S(2)}) collective-permute-start(bf16[512,128]{1,0:T(8,128)(2,1)S(1)} %get-tuple-element.13), channel_id=1, source_target_pairs={{0,2},{1,3},{2,0},{3,1},{4,6},{5,7},{6,4},{7,5},{8,10},{9,11},{10,... | collective-permute-start | bytes 393224 | tf_op jit(solution)/shard_map/ppermute | solution.py:445
  46.4 4.0 %collective-permute-start.1 = (bf16[16,120,128]{2,1,0:T(8,128)(2,1)S(1)}, bf16[16,120,128]{2,1,0:T(8,128)(2,1)S(1)}, u32[]{:S(2)}, u32[]{:S(2)}) collective-permute-start(bf16[16,120,128]{2,1,0:T(8,128)(2,1)S(1)} %all_to_all.11.mine_ref), channel_id=1, source_target_pairs={{0,1},{1,0},{2,3},{3,2},{4,5},{5,4},{6,7},{7,6},{8,9},{9,8},{10,11... | collective-permute-start | bytes 1474568 | tf_op jit(solution)/shard_map/ppermute | solution.py:449
  51.7 3.2 %collective-permute-start.2 = (bf16[272,128]{1,0:T(8,128)(2,1)S(1)}, bf16[272,128]{1,0:T(8,128)(2,1)S(1)}, u32[]{:S(2)}, u32[]{:S(2)}) collective-permute-start(bf16[272,128]{1,0:T(8,128)(2,1)S(1)} %attend_far.1), channel_id=1, source_target_pairs={{0,2},{1,3},{2,0},{3,1},{4,6},{5,7},{6,4},{7,5},{8,10},{9,11},{10,... | collective-permute-start | bytes 208904 | tf_op jit(solution)/shard_map/ppermute | solution.py:464

commit v5 on v4

--- a/solution.py
+++ b/solution.py
@@ -23,7 +23,11 @@
 KEYS = HALF_TOK + HALF_IMG
 TAIL = 16
 PAY = KEYS + 2 * TAIL
-TILES = N_SEQ // 2 + N_SEQ // 4
+PAIRS = N_SEQ // 2
+TILES = PAIRS + N_SEQ // 4
+MOST_DOC = 1152
+REACH = MOST_DOC // TOK
+WINDOW = REACH // 2 + 2
 DOCS = 32
 KCH = 4
 LIMIT = 60 << 20
@@ -125,6 +129,20 @@
             upper, table[TOK + HALF_IMG :], table[TOK : TOK + HALF_IMG]
         )
 
+    for copy in small[3:] + copies[2:4]:
+        copy.wait()
+    queries = jnp.broadcast_to(bqs[...].astype(f32).reshape(1, 2 * HD), (ROWS, 2 * HD))
+    kv = jnp.zeros((ROWS, 64), f32)
+    for c in range(KCH):
+        if c % 2 == 0:
+            copies[4 + c].wait()
+            copies[5 + c].wait()
+        part = pl.ds(c * step, step)
+        gain = gains[part].astype(f32).reshape(1, step)
+        normed = (xs[:, part].astype(f32) * inverse * gain).astype(bf16)
+        kv = kv + dot_t(normed, wkvs[:, part])
+        queries = queries + jnp.dot(normed, wqs[part, :], preferred_element_type=f32)
+
     earlier = iota((IMG, IMG), 0) < iota((IMG, IMG), 1)
     later = iota((IMG, IMG), 0) > iota((IMG, IMG), 1)
     same = hi_col == hi_row
@@ -145,20 +163,6 @@
     lo_two = jnp.sum(jnp.where(spread, lo_col, 0.0), axis=0, keepdims=True)
     wide_slot = iota((count, HD), 0) % TAIL
     tail = tail + jnp.where(wide_slot == 12, hi_two, jnp.where(wide_slot == 13, lo_two, 0.0))
-
-    for copy in small[3:] + copies[2:4]:
-        copy.wait()
-    queries = jnp.broadcast_to(bqs[...].astype(f32).reshape(1, 2 * HD), (ROWS, 2 * HD))
-    kv = jnp.zeros((ROWS, 64), f32)
-    for c in range(KCH):
-        if c % 2 == 0:
-            copies[4 + c].wait()
-            copies[5 + c].wait()
-        part = pl.ds(c * step, step)
-        gain = gains[part].astype(f32).reshape(1, step)
-        normed = (xs[:, part].astype(f32) * inverse * gain).astype(bf16)
-        kv = kv + dot_t(normed, wkvs[:, part])
-        queries = queries + jnp.dot(normed, wqs[part, :], preferred_element_type=f32)
 
     kv = jnp.concatenate([kv, jnp.zeros((ROWS, 64), f32)], axis=1)
     eye8 = iota((8, 8), 0) == iota((8, 8), 1)
@@ -275,19 +279,29 @@
     first = (lax.axis_index("seq") * TOK).astype(f32)
     slope = math.log2(math.e) / math.sqrt(HD)
 
+    low = jnp.maximum(lax.axis_index("seq") - REACH, 0) // 2
+    low = jnp.minimum(low, PAIRS - WINDOW)
+
     def tile_of(ref, t):
-        if t < N_SEQ // 2:
-            return ref[2 * t : 2 * t + 2, 0:HALF_TOK, :].reshape(HD, HD)
-        m = t - N_SEQ // 2
+        if t < WINDOW:
+            return ref[pl.ds(2 * (low + t), 2), 0:HALF_TOK, :].reshape(HD, HD)
+        m = t - WINDOW
         return ref[4 * m : 4 * m + 4, HALF_TOK : HALF_TOK + 32, :].reshape(HD, HD)
+
+    def where_of(t):
+        if t < WINDOW:
+            return where_ref[pl.ds(low + t, 1), :]
+        return where_ref[PAIRS + t - WINDOW : PAIRS + t - WINDOW + 1, :]
+
+    steps = WINDOW + N_SEQ // 4
 
     def attend(keys, values):
         queries = q_ref[count:, :] if far else q_ref[:count, :]
         position = first + fiota((TOK, HD), 0)
         start = start_ref[...]
         top = jnp.full((count, HD), NEG, f32)
-        for t in range(TILES):
-            where = where_ref[t : t + 1, :]
+        for t in range(steps):
+            where = where_of(t)
             allowed = (where <= position) & (where >= start)
             allowed = jnp.concatenate([allowed] * 2, axis=0)
             score = jnp.where(allowed, dot_t(queries, tile_of(keys, t)), NEG)
@@ -296,7 +310,7 @@
         top = jnp.maximum(jnp.max(top, axis=1, keepdims=True), LOW)
         total = jnp.zeros((count, HD), f32)
         mix = jnp.zeros((count, HD), f32)
-        for t in range(TILES):
+        for t in range(steps):
             weight = jnp.exp2((scores[t] - top) * slope)
             total = total + weight
             mix = mix + jnp.dot(weight.astype(bf16), tile_of(values, t), preferred_element_type=f32)
@@ -400,7 +414,7 @@
         out_shape=jax.ShapeDtypeStruct(*out),
         in_specs=[vmem()] * 5,
         out_specs=vmem(),
-        scratch_shapes=[pltpu.VMEM((TILES, 2 * TOK, HD), f32)],
+        scratch_shapes=[pltpu.VMEM((WINDOW + N_SEQ // 4, 2 * TOK, HD), f32)],
         compiler_params=small_params(),
         cost_estimate=pl.CostEstimate(flops=1 << 30, bytes_accessed=1 << 21, transcendentals=1 << 19),
     )

time: 55.9 us -> 55.6 us (level)
  transfers between devices with their start and end apart: 3 -> 3, of which waited for: 2 -> 2; matrix products, arithmetic and copies ran while one was open for 0% -> 0% of each run, Pallas kernels for 5% -> 4%
where the time goes in v5:
time: 55.6 us; the launch traced here: 55.4 us
  blocking collectives  38.8 us (70%)
  Pallas kernels  9.53 us (17%)
  starting transfers between devices  5.13 us (9%)
  waiting for transfers between devices  1.98 us (4%)
    all_to_all x1, blocking collectives, body(): mine = lax.all_to_all(payload, 'seq', 0, 0)  27.1 us
    all_to_all x1, blocking collectives, body(): kv_mine = lax.all_to_all(kv_send, 'head', 0, 0)  11.7 us
    pallas_call x1, Pallas kernels, project_call(): call(*(pltpu.with_memory_space_constraint(array, pltpu.HBM) for array in...  5.11 us
    ppermute x1, starting transfers between devices, body(): other = lax.ppermute(mine, 'head', core_swap)  2.54 us
    ppermute x1, starting transfers between devices, body(): shared = lax.ppermute(share, 'head', chip_swap)  2.21 us
    ppermute x1, waiting for transfers between devices, body(): come = lax.ppermute(send, 'head', chip_swap)  1.75 us
    pallas_call x1, Pallas kernels, body(): pl.pallas_call(place_kernel, name='place', out_shape=(jax.ShapeDtypeStruc...  1.26 us
    pallas_call x1, Pallas kernels, body(): keep = attend_call(False)(merged, where, start, mine, other)  1.12 us
  transfers between devices with their start and end apart: 3, of which 2 were waited for; matrix products, arithmetic and copies ran while one was open for 0% of the time, Pallas kernels for 4%

profile of v5, /device:TPU:1, one launch (start us, length us, event | category | flops | bytes accessed | tf_op | source)
XLA Modules:
  0.0 55.4 jit_solution(1740389542929909015)
XLA Ops:
  0.0 0.0 copy-start
  0.0 5.1 %project.1 = (bf16[16,8,128]{2,1,0:T(8,128)(2,1)S(1)}, bf16[512,128]{1,0:T(8,128)(2,1)S(1)}, f32[432,128]{1,0:T(8,128)S(1)}, f32[384,128]{1,0:T(8,128)S(1)}) custom-call(bf16[128,8192]{1,0:T(8,128)(2,1)} %x_hbm.1, bf16[48,8192]{1,0:T(8,128)(2,1)} %img_hbm.1, bf16[8192,256]{1,0:T(8,128)(2,1)} %wq_hbm.1, bf16[32,8192]{1,0:T(8,128)(2,1)} %bitcast.7, ...), custom_call_target="tpu_custom_call" | custom-call | tf_op jit(solution)/shard_map/project/pallas_call | solution.py:404
  5.1 2.2 %collective-permute-start = (bf16[512,128]{1,0:T(8,128)(2,1)S(1)}, bf16[512,128]{1,0:T(8,128)(2,1)S(1)}, u32[]{:S(2)}, u32[]{:S(2)}) collective-permute-start(bf16[512,128]{1,0:T(8,128)(2,1)S(1)} %get-tuple-element.13), channel_id=1, source_target_pairs={{0,2},{1,3},{2,0},{3,1},{4,6},{5,7},{6,4},{7,5},{8,10},{9,11},{10,... | collective-permute-start | bytes 393224 | tf_op jit(solution)/shard_map/ppermute | solution.py:459
  7.3 11.7 %all_to_all.10.kv_ref = bf16[16,8,128]{2,1,0:T(8,128)(2,1)S(1)} all-to-all(bf16[16,8,128]{2,1,0:T(8,128)(2,1)S(1)} %get-tuple-element.14), channel_id=1, replica_groups=mesh['seq'=16,'head'=16] {'head'}, dimensions={0} | all-to-all | bytes 65536 | tf_op jit(solution)/shard_map/all_to_all | solution.py:460
  19.0 0.0 collective-permute-done.share_ref
  19.0 0.2 panel.1
  19.2 27.1 %all_to_all.11.mine_ref = bf16[16,120,128]{2,1,0:T(8,128)(2,1)S(1)} all-to-all(bf16[16,120,128]{2,1,0:T(8,128)(2,1)S(1)} %panel.1), channel_id=1, replica_groups=mesh['seq'=16,'head'=16] {'seq'}, dimensions={0} | all-to-all | bytes 983040 | tf_op jit(solution)/shard_map/all_to_all | solution.py:462
  46.3 2.5 %collective-permute-start.1 = (bf16[16,120,128]{2,1,0:T(8,128)(2,1)S(1)}, bf16[16,120,128]{2,1,0:T(8,128)(2,1)S(1)}, u32[]{:S(2)}, u32[]{:S(2)}) collective-permute-start(bf16[16,120,128]{2,1,0:T(8,128)(2,1)S(1)} %all_to_all.11.mine_ref), channel_id=1, source_target_pairs={{0,1},{1,0},{2,3},{3,2},{4,5},{5,4},{6,7},{7,6},{8,9},{9,8},{10,11... | collective-permute-start | bytes 1474568 | tf_op jit(solution)/shard_map/ppermute | solution.py:463
  48.8 0.0 copy-done
  48.8 1.3 %place.1 = (bf16[512,128]{1,0:T(8,128)(2,1)S(1)}, f32[12,128]{1,0:T(8,128)S(1)}, f32[128,128]{1,0:T(8,128)S(1)}) custom-call(f32[384,128]{1,0:T(8,128)S(1)} %get-tuple-element.12.own_ref, bf16[512,128]{1,0:T(8,128)(2,1)S(1)} %collective-permute-done.share_ref, bf16[16,120,128]{2,1,0:T(8,128)(2,1)S(1)} %all_to_all.11.mine_ref, s32[1,16]{1,0:T(1,128)S(1)} %copy-done), custom_call_target="tpu_custom_call" | custom-call | flops 268435456 | bytes 1048576 | tf_op jit(solution)/shard_map/place/pallas_call | solution.py:464
  50.1 0.2 collective-permute-done.1.other_ref
  50.3 1.1 %attend_far.1 = bf16[272,128]{1,0:T(8,128)(2,1)S(1)} custom-call(bf16[512,128]{1,0:T(8,128)(2,1)S(1)} %get-tuple-element.16.q_ref, f32[12,128]{1,0:T(8,128)S(1)} %get-tuple-element.17.where_ref, f32[128,128]{1,0:T(8,128)S(1)} %get-tuple-element.18.start_ref, bf16[16,120,128]{2,1,0:T(8,128)(2,1)S(1)} %all_to_all.11.mine_ref, ...), custom_call_target="tpu_custom_call" | custom-call | flops 1073741824 | bytes 2097152 | tf_op jit(solution)/shard_map/attend_far/pallas_call | solution.py:477
  51.4 0.4 collective-permute-start.2
  51.8 1.1 %attend_near.1.keep_ref = f32[3,256,128]{2,1,0:T(8,128)S(1)} custom-call(bf16[512,128]{1,0:T(8,128)(2,1)S(1)} %get-tuple-element.16.q_ref, f32[12,128]{1,0:T(8,128)S(1)} %get-tuple-element.17.where_ref, f32[128,128]{1,0:T(8,128)S(1)} %get-tuple-element.18.start_ref, bf16[16,120,128]{2,1,0:T(8,128)(2,1)S(1)} %all_to_all.11.mine_ref, ...), custom_call_target="tpu_custom_call" | custom-call | flops 1073741824 | bytes 2097152 | tf_op jit(solution)/shard_map/attend_near/pallas_call | solution.py:479
  52.9 1.7 %collective-permute-done.2.come_ref = bf16[272,128]{1,0:T(8,128)(2,1)S(1)} collective-permute-done((bf16[272,128]{1,0:T(8,128)(2,1)S(1)}, bf16[272,128]{1,0:T(8,128)(2,1)S(1)}, u32[]{:S(2)}, u32[]{:S(2)}) %collective-permute-start.2) | collective-permute-done | bytes 69664 | tf_op jit(solution)/shard_map/ppermute | solution.py:478
  54.6 0.8 %combine.1 = bf16[128,256]{1,0:T(8,128)(2,1)} custom-call(f32[3,256,128]{2,1,0:T(8,128)S(1)} %attend_near.1.keep_ref, bf16[272,128]{1,0:T(8,128)(2,1)S(1)} %collective-permute-done.2.come_ref), custom_call_target="tpu_custom_call" | custom-call | tf_op jit(solution)/shard_map/combine/pallas_call | solution.py:480
Async XLA Ops:
  0.0 48.8 %copy-start = (s32[1,16]{1,0:T(1,128)S(1)}, s32[1,16]{1,0:T(1,128)}, u32[]{:S(2)}) copy-start(s32[1,16]{1,0:T(1,128)} %mask_ref.1) | copy-start | bytes 196
  5.1 13.9 %collective-permute-start = (bf16[512,128]{1,0:T(8,128)(2,1)S(1)}, bf16[512,128]{1,0:T(8,128)(2,1)S(1)}, u32[]{:S(2)}, u32[]{:S(2)}) collective-permute-start(bf16[512,128]{1,0:T(8,128)(2,1)S(1)} %get-tuple-element.13), channel_id=1, source_target_pairs={{0,2},{1,3},{2,0},{3,1},{4,6},{5,7},{6,4},{7,5},{8,10},{9,11},{10,... | collective-permute-start | bytes 393224 | tf_op jit(solution)/shard_map/ppermute | solution.py:459
  46.3 4.0 %collective-permute-start.1 = (bf16[16,120,128]{2,1,0:T(8,128)(2,1)S(1)}, bf16[16,120,128]{2,1,0:T(8,128)(2,1)S(1)}, u32[]{:S(2)}, u32[]{:S(2)}) collective-permute-start(bf16[16,120,128]{2,1,0:T(8,128)(2,1)S(1)} %all_to_all.11.mine_ref), channel_id=1, source_target_pairs={{0,1},{1,0},{2,3},{3,2},{4,5},{5,4},{6,7},{7,6},{8,9},{9,8},{10,11... | collective-permute-start | bytes 1474568 | tf_op jit(solution)/shard_map/ppermute | solution.py:463
  51.4 3.2 %collective-permute-start.2 = (bf16[272,128]{1,0:T(8,128)(2,1)S(1)}, bf16[272,128]{1,0:T(8,128)(2,1)S(1)}, u32[]{:S(2)}, u32[]{:S(2)}) collective-permute-start(bf16[272,128]{1,0:T(8,128)(2,1)S(1)} %attend_far.1), channel_id=1, source_target_pairs={{0,2},{1,3},{2,0},{3,1},{4,6},{5,7},{6,4},{7,5},{8,10},{9,11},{10,... | collective-permute-start | bytes 208904 | tf_op jit(solution)/shard_map/ppermute | solution.py:478

commit v6 on v5

--- a/solution.py
+++ b/solution.py
@@ -24,7 +24,6 @@
 TAIL = 16
 PAY = KEYS + 2 * TAIL
 PAIRS = N_SEQ // 2
-TILES = PAIRS + N_SEQ // 4
 MOST_DOC = 1152
 REACH = MOST_DOC // TOK
 WINDOW = REACH // 2 + 2
@@ -108,14 +107,20 @@
     lo_row = dest_row - TOK * hi_row
     lo_col = dest_col - TOK * hi_col
 
-    index_col = jnp.concatenate([first + fiota((TOK, 1), 0), dest_col], axis=0)
-    start_col = jnp.zeros((ROWS, 1), f32)
+    token_row = first + fiota((1, TOK), 1)
+    token_start = jnp.zeros((1, TOK), f32)
+    image_start = jnp.zeros((1, IMG), f32)
     begin = jnp.int32(0)
     for d in range(DOCS):
         begin_f = begin.astype(f32)
-        start_col = jnp.where(index_col >= begin_f, begin_f, start_col)
+        token_start = jnp.where(token_row >= begin_f, begin_f, token_start)
+        image_start = jnp.where(dest_row >= begin_f, begin_f, image_start)
         begin = begin + docs_ref[d]
-    own[2 * TOK :, :] = jnp.broadcast_to(start_col[:TOK], (TOK, HD))
+    image_start = jnp.sum(jnp.where(eye, image_start, 0.0), axis=1, keepdims=True)
+    token_start = jnp.transpose(jnp.broadcast_to(token_start, (TOK, TOK)))
+    index_col = jnp.concatenate([first + fiota((TOK, HD), 0), jnp.broadcast_to(dest_col, (IMG, HD))], axis=0)
+    start_col = jnp.concatenate([token_start, jnp.broadcast_to(image_start, (IMG, HD))], axis=0)
+    own[2 * TOK :, :] = start_col[:TOK]
     angles = (index_col - start_col) * invfs[...]
     cosine = jnp.cos(angles)
     sine = jnp.sin(angles)
@@ -466,7 +471,7 @@
         name="place",
         out_shape=(
             jax.ShapeDtypeStruct((4 * TOK, HD), bf16),
-            jax.ShapeDtypeStruct((TILES, HD), f32),
+            jax.ShapeDtypeStruct((N_SEQ, HD), f32),
             jax.ShapeDtypeStruct((TOK, HD), f32),
         ),
         in_specs=[vmem()] * 3 + [smem],

time: 55.6 us -> 55.5 us (level)
  no operation moved by 1% of the time
where the time goes in v6:
time: 55.5 us; the launch traced here: 55.3 us
  blocking collectives  38.8 us (70%)
  Pallas kernels  9.44 us (17%)
  starting transfers between devices  5.12 us (9%)
  waiting for transfers between devices  1.98 us (4%)
    all_to_all x1, blocking collectives, body(): mine = lax.all_to_all(payload, 'seq', 0, 0)  27.1 us
    all_to_all x1, blocking collectives, body(): kv_mine = lax.all_to_all(kv_send, 'head', 0, 0)  11.7 us
    pallas_call x1, Pallas kernels, project_call(): call(*(pltpu.with_memory_space_constraint(array, pltpu.HBM) for array in...  5.02 us
    ppermute x1, starting transfers between devices, body(): other = lax.ppermute(mine, 'head', core_swap)  2.54 us
    ppermute x1, starting transfers between devices, body(): shared = lax.ppermute(share, 'head', chip_swap)  2.2 us
    ppermute x1, waiting for transfers between devices, body(): come = lax.ppermute(send, 'head', chip_swap)  1.75 us
    pallas_call x1, Pallas kernels, body(): pl.pallas_call(place_kernel, name='place', out_shape=(jax.ShapeDtypeStruc...  1.26 us
    pallas_call x1, Pallas kernels, body(): keep = attend_call(False)(merged, where, start, mine, other)  1.12 us
  transfers between devices with their start and end apart: 3, of which 2 were waited for; matrix products, arithmetic and copies ran while one was open for 0% of the time, Pallas kernels for 4%

profile of v6, /device:TPU:1, one launch (start us, length us, event | category | flops | bytes accessed | tf_op | source)
XLA Modules:
  0.0 55.3 jit_solution(10355232275981399815)
XLA Ops:
  0.0 0.0 copy-start
  0.0 5.0 %project.1 = (bf16[16,8,128]{2,1,0:T(8,128)(2,1)S(1)}, bf16[512,128]{1,0:T(8,128)(2,1)S(1)}, f32[432,128]{1,0:T(8,128)S(1)}, f32[384,128]{1,0:T(8,128)S(1)}) custom-call(bf16[128,8192]{1,0:T(8,128)(2,1)} %x_hbm.1, bf16[48,8192]{1,0:T(8,128)(2,1)} %img_hbm.1, bf16[8192,256]{1,0:T(8,128)(2,1)} %wq_hbm.1, bf16[32,8192]{1,0:T(8,128)(2,1)} %bitcast.7, ...), custom_call_target="tpu_custom_call" | custom-call | tf_op jit(solution)/shard_map/project/pallas_call | solution.py:409
  5.0 2.2 %collective-permute-start = (bf16[512,128]{1,0:T(8,128)(2,1)S(1)}, bf16[512,128]{1,0:T(8,128)(2,1)S(1)}, u32[]{:S(2)}, u32[]{:S(2)}) collective-permute-start(bf16[512,128]{1,0:T(8,128)(2,1)S(1)} %get-tuple-element.13), channel_id=1, source_target_pairs={{0,2},{1,3},{2,0},{3,1},{4,6},{5,7},{6,4},{7,5},{8,10},{9,11},{10,... | collective-permute-start | bytes 393224 | tf_op jit(solution)/shard_map/ppermute | solution.py:464
  7.2 11.7 %all_to_all.10.kv_ref = bf16[16,8,128]{2,1,0:T(8,128)(2,1)S(1)} all-to-all(bf16[16,8,128]{2,1,0:T(8,128)(2,1)S(1)} %get-tuple-element.14), channel_id=1, replica_groups=mesh['seq'=16,'head'=16] {'head'}, dimensions={0} | all-to-all | bytes 65536 | tf_op jit(solution)/shard_map/all_to_all | solution.py:465
  18.9 0.0 collective-permute-done.share_ref
  18.9 0.2 panel.1
  19.1 27.1 %all_to_all.11.mine_ref = bf16[16,120,128]{2,1,0:T(8,128)(2,1)S(1)} all-to-all(bf16[16,120,128]{2,1,0:T(8,128)(2,1)S(1)} %panel.1), channel_id=1, replica_groups=mesh['seq'=16,'head'=16] {'seq'}, dimensions={0} | all-to-all | bytes 983040 | tf_op jit(solution)/shard_map/all_to_all | solution.py:467
  46.2 2.5 %collective-permute-start.1 = (bf16[16,120,128]{2,1,0:T(8,128)(2,1)S(1)}, bf16[16,120,128]{2,1,0:T(8,128)(2,1)S(1)}, u32[]{:S(2)}, u32[]{:S(2)}) collective-permute-start(bf16[16,120,128]{2,1,0:T(8,128)(2,1)S(1)} %all_to_all.11.mine_ref), channel_id=1, source_target_pairs={{0,1},{1,0},{2,3},{3,2},{4,5},{5,4},{6,7},{7,6},{8,9},{9,8},{10,11... | collective-permute-start | bytes 1474568 | tf_op jit(solution)/shard_map/ppermute | solution.py:468
  48.7 0.0 copy-done
  48.7 1.3 %place.1 = (bf16[512,128]{1,0:T(8,128)(2,1)S(1)}, f32[16,128]{1,0:T(8,128)S(1)}, f32[128,128]{1,0:T(8,128)S(1)}) custom-call(f32[384,128]{1,0:T(8,128)S(1)} %get-tuple-element.12.own_ref, bf16[512,128]{1,0:T(8,128)(2,1)S(1)} %collective-permute-done.share_ref, bf16[16,120,128]{2,1,0:T(8,128)(2,1)S(1)} %all_to_all.11.mine_ref, s32[1,16]{1,0:T(1,128)S(1)} %copy-done), custom_call_target="tpu_custom_call" | custom-call | flops 268435456 | bytes 1048576 | tf_op jit(solution)/shard_map/place/pallas_call | solution.py:469
  50.0 0.2 collective-permute-done.1.other_ref
  50.2 1.1 %attend_far.1 = bf16[272,128]{1,0:T(8,128)(2,1)S(1)} custom-call(bf16[512,128]{1,0:T(8,128)(2,1)S(1)} %get-tuple-element.16.q_ref, f32[16,128]{1,0:T(8,128)S(1)} %get-tuple-element.17.where_ref, f32[128,128]{1,0:T(8,128)S(1)} %get-tuple-element.18.start_ref, bf16[16,120,128]{2,1,0:T(8,128)(2,1)S(1)} %all_to_all.11.mine_ref, ...), custom_call_target="tpu_custom_call" | custom-call | flops 1073741824 | bytes 2097152 | tf_op jit(solution)/shard_map/attend_far/pallas_call | solution.py:482
  51.3 0.4 collective-permute-start.2
  51.7 1.1 %attend_near.1.keep_ref = f32[3,256,128]{2,1,0:T(8,128)S(1)} custom-call(bf16[512,128]{1,0:T(8,128)(2,1)S(1)} %get-tuple-element.16.q_ref, f32[16,128]{1,0:T(8,128)S(1)} %get-tuple-element.17.where_ref, f32[128,128]{1,0:T(8,128)S(1)} %get-tuple-element.18.start_ref, bf16[16,120,128]{2,1,0:T(8,128)(2,1)S(1)} %all_to_all.11.mine_ref, ...), custom_call_target="tpu_custom_call" | custom-call | flops 1073741824 | bytes 2097152 | tf_op jit(solution)/shard_map/attend_near/pallas_call | solution.py:484
  52.8 1.7 %collective-permute-done.2.come_ref = bf16[272,128]{1,0:T(8,128)(2,1)S(1)} collective-permute-done((bf16[272,128]{1,0:T(8,128)(2,1)S(1)}, bf16[272,128]{1,0:T(8,128)(2,1)S(1)}, u32[]{:S(2)}, u32[]{:S(2)}) %collective-permute-start.2) | collective-permute-done | bytes 69664 | tf_op jit(solution)/shard_map/ppermute | solution.py:483
  54.5 0.8 %combine.1 = bf16[128,256]{1,0:T(8,128)(2,1)} custom-call(f32[3,256,128]{2,1,0:T(8,128)S(1)} %attend_near.1.keep_ref, bf16[272,128]{1,0:T(8,128)(2,1)S(1)} %collective-permute-done.2.come_ref), custom_call_target="tpu_custom_call" | custom-call | tf_op jit(solution)/shard_map/combine/pallas_call | solution.py:485
Async XLA Ops:
  0.0 48.7 %copy-start = (s32[1,16]{1,0:T(1,128)S(1)}, s32[1,16]{1,0:T(1,128)}, u32[]{:S(2)}) copy-start(s32[1,16]{1,0:T(1,128)} %mask_ref.1) | copy-start | bytes 196
  5.0 13.9 %collective-permute-start = (bf16[512,128]{1,0:T(8,128)(2,1)S(1)}, bf16[512,128]{1,0:T(8,128)(2,1)S(1)}, u32[]{:S(2)}, u32[]{:S(2)}) collective-permute-start(bf16[512,128]{1,0:T(8,128)(2,1)S(1)} %get-tuple-element.13), channel_id=1, source_target_pairs={{0,2},{1,3},{2,0},{3,1},{4,6},{5,7},{6,4},{7,5},{8,10},{9,11},{10,... | collective-permute-start | bytes 393224 | tf_op jit(solution)/shard_map/ppermute | solution.py:464
  46.2 4.0 %collective-permute-start.1 = (bf16[16,120,128]{2,1,0:T(8,128)(2,1)S(1)}, bf16[16,120,128]{2,1,0:T(8,128)(2,1)S(1)}, u32[]{:S(2)}, u32[]{:S(2)}) collective-permute-start(bf16[16,120,128]{2,1,0:T(8,128)(2,1)S(1)} %all_to_all.11.mine_ref), channel_id=1, source_target_pairs={{0,1},{1,0},{2,3},{3,2},{4,5},{5,4},{6,7},{7,6},{8,9},{9,8},{10,11... | collective-permute-start | bytes 1474568 | tf_op jit(solution)/shard_map/ppermute | solution.py:468
  51.3 3.2 %collective-permute-start.2 = (bf16[272,128]{1,0:T(8,128)(2,1)S(1)}, bf16[272,128]{1,0:T(8,128)(2,1)S(1)}, u32[]{:S(2)}, u32[]{:S(2)}) collective-permute-start(bf16[272,128]{1,0:T(8,128)(2,1)S(1)} %attend_far.1), channel_id=1, source_target_pairs={{0,2},{1,3},{2,0},{3,1},{4,6},{5,7},{6,4},{7,5},{8,10},{9,11},{10,... | collective-permute-start | bytes 208904 | tf_op jit(solution)/shard_map/ppermute | solution.py:483

commit v7 on v5

--- a/solution.py
+++ b/solution.py
@@ -344,7 +344,7 @@
         attend(other_ref, mine_ref)
 
 
-def combine_kernel(keep_ref, come_ref, out_ref):
+def combine_kernel(keep_ref, come_ref, out_hbm, halves, sems):
     slope = math.log2(math.e) / math.sqrt(HD)
     pieces = come_ref[2 * TOK :, :].astype(f32)
 
@@ -352,6 +352,7 @@
         row = pieces[3 * i : 3 * i + 1] + pieces[3 * i + 1 : 3 * i + 2] + pieces[3 * i + 2 : 3 * i + 3]
         return jnp.transpose(jnp.broadcast_to(row, (TOK, HD)))
 
+    copies = []
     for e in range(2):
         span = slice(e * TOK, (e + 1) * TOK)
         top_near = keep_ref[1, span, :]
@@ -360,7 +361,15 @@
         near = jnp.exp2((top_near - top) * slope)
         far = jnp.exp2((top_far - top) * slope) * column(2 + e)
         mix = keep_ref[0, span, :] * near + come_ref[span, :].astype(f32) * far
-        out_ref[:, e * HD : (e + 1) * HD] = (mix / (keep_ref[2, span, :] * near + far)).astype(bf16)
+        halves[e] = (mix / (keep_ref[2, span, :] * near + far)).astype(bf16)
+        copies.append(
+            pltpu.make_async_copy(
+                halves.at[e], out_hbm.at[:, pl.ds(e * HD, HD)], sems.at[e]
+            )
+        )
+        copies[e].start()
+    for copy in copies:
+        copy.wait()
 
 
 def vmem():
@@ -482,7 +491,8 @@
         name="combine",
         out_shape=jax.ShapeDtypeStruct((TOK, 2 * HD), bf16),
         in_specs=[vmem()] * 2,
-        out_specs=vmem(),
+        out_specs=pl.BlockSpec(memory_space=pltpu.HBM),
+        scratch_shapes=[pltpu.VMEM((2, TOK, HD), bf16), pltpu.SemaphoreType.DMA((2,))],
         compiler_params=small_params(),
     )(keep, come)
 

time: 55.6 us -> 55.6 us (level)
  no operation moved by 1% of the time
where the time goes in v7:
time: 55.6 us; the launch traced here: 55.4 us
  blocking collectives  38.8 us (70%)
  Pallas kernels  9.54 us (17%)
  starting transfers between devices  5.13 us (9%)
  waiting for transfers between devices  1.98 us (4%)
    all_to_all x1, blocking collectives, body(): mine = lax.all_to_all(payload, 'seq', 0, 0)  27.1 us
    all_to_all x1, blocking collectives, body(): kv_mine = lax.all_to_all(kv_send, 'head', 0, 0)  11.7 us
    pallas_call x1, Pallas kernels, project_call(): call(*(pltpu.with_memory_space_constraint(array, pltpu.HBM) for array in...  5.11 us
    ppermute x1, starting transfers between devices, body(): other = lax.ppermute(mine, 'head', core_swap)  2.54 us
    ppermute x1, starting transfers between devices, body(): shared = lax.ppermute(share, 'head', chip_swap)  2.21 us
    ppermute x1, waiting for transfers between devices, body(): come = lax.ppermute(send, 'head', chip_swap)  1.75 us
    pallas_call x1, Pallas kernels, body(): pl.pallas_call(place_kernel, name='place', out_shape=(jax.ShapeDtypeStruc...  1.26 us
    pallas_call x1, Pallas kernels, body(): keep = attend_call(False)(merged, where, start, mine, other)  1.12 us
  transfers between devices with their start and end apart: 3, of which 2 were waited for; matrix products, arithmetic and copies ran while one was open for 0% of the time, Pallas kernels for 4%

profile of v7, /device:TPU:1, one launch (start us, length us, event | category | flops | bytes accessed | tf_op | source)
XLA Modules:
  0.0 55.4 jit_solution(9723396348428190268)
XLA Ops:
  0.0 0.0 copy-start
  0.0 5.1 %project.1 = (bf16[16,8,128]{2,1,0:T(8,128)(2,1)S(1)}, bf16[512,128]{1,0:T(8,128)(2,1)S(1)}, f32[432,128]{1,0:T(8,128)S(1)}, f32[384,128]{1,0:T(8,128)S(1)}) custom-call(bf16[128,8192]{1,0:T(8,128)(2,1)} %x_hbm.1, bf16[48,8192]{1,0:T(8,128)(2,1)} %img_hbm.1, bf16[8192,256]{1,0:T(8,128)(2,1)} %wq_hbm.1, bf16[32,8192]{1,0:T(8,128)(2,1)} %bitcast.7, ...), custom_call_target="tpu_custom_call" | custom-call | tf_op jit(solution)/shard_map/project/pallas_call | solution.py:413
  5.1 2.2 %collective-permute-start = (bf16[512,128]{1,0:T(8,128)(2,1)S(1)}, bf16[512,128]{1,0:T(8,128)(2,1)S(1)}, u32[]{:S(2)}, u32[]{:S(2)}) collective-permute-start(bf16[512,128]{1,0:T(8,128)(2,1)S(1)} %get-tuple-element.13), channel_id=1, source_target_pairs={{0,2},{1,3},{2,0},{3,1},{4,6},{5,7},{6,4},{7,5},{8,10},{9,11},{10,... | collective-permute-start | bytes 393224 | tf_op jit(solution)/shard_map/ppermute | solution.py:468
  7.3 11.7 %all_to_all.10.kv_ref = bf16[16,8,128]{2,1,0:T(8,128)(2,1)S(1)} all-to-all(bf16[16,8,128]{2,1,0:T(8,128)(2,1)S(1)} %get-tuple-element.14), channel_id=1, replica_groups=mesh['seq'=16,'head'=16] {'head'}, dimensions={0} | all-to-all | bytes 65536 | tf_op jit(solution)/shard_map/all_to_all | solution.py:469
  19.0 0.0 collective-permute-done.share_ref
  19.0 0.2 panel.1
  19.2 27.1 %all_to_all.11.mine_ref = bf16[16,120,128]{2,1,0:T(8,128)(2,1)S(1)} all-to-all(bf16[16,120,128]{2,1,0:T(8,128)(2,1)S(1)} %panel.1), channel_id=1, replica_groups=mesh['seq'=16,'head'=16] {'seq'}, dimensions={0} | all-to-all | bytes 983040 | tf_op jit(solution)/shard_map/all_to_all | solution.py:471
  46.3 2.5 %collective-permute-start.1 = (bf16[16,120,128]{2,1,0:T(8,128)(2,1)S(1)}, bf16[16,120,128]{2,1,0:T(8,128)(2,1)S(1)}, u32[]{:S(2)}, u32[]{:S(2)}) collective-permute-start(bf16[16,120,128]{2,1,0:T(8,128)(2,1)S(1)} %all_to_all.11.mine_ref), channel_id=1, source_target_pairs={{0,1},{1,0},{2,3},{3,2},{4,5},{5,4},{6,7},{7,6},{8,9},{9,8},{10,11... | collective-permute-start | bytes 1474568 | tf_op jit(solution)/shard_map/ppermute | solution.py:472
  48.8 0.0 copy-done
  48.8 1.3 %place.1 = (bf16[512,128]{1,0:T(8,128)(2,1)S(1)}, f32[12,128]{1,0:T(8,128)S(1)}, f32[128,128]{1,0:T(8,128)S(1)}) custom-call(f32[384,128]{1,0:T(8,128)S(1)} %get-tuple-element.12.own_ref, bf16[512,128]{1,0:T(8,128)(2,1)S(1)} %collective-permute-done.share_ref, bf16[16,120,128]{2,1,0:T(8,128)(2,1)S(1)} %all_to_all.11.mine_ref, s32[1,16]{1,0:T(1,128)S(1)} %copy-done), custom_call_target="tpu_custom_call" | custom-call | flops 268435456 | bytes 1048576 | tf_op jit(solution)/shard_map/place/pallas_call | solution.py:473
  50.1 0.2 collective-permute-done.1.other_ref
  50.3 1.1 %attend_far.1 = bf16[272,128]{1,0:T(8,128)(2,1)S(1)} custom-call(bf16[512,128]{1,0:T(8,128)(2,1)S(1)} %get-tuple-element.16.q_ref, f32[12,128]{1,0:T(8,128)S(1)} %get-tuple-element.17.where_ref, f32[128,128]{1,0:T(8,128)S(1)} %get-tuple-element.18.start_ref, bf16[16,120,128]{2,1,0:T(8,128)(2,1)S(1)} %all_to_all.11.mine_ref, ...), custom_call_target="tpu_custom_call" | custom-call | flops 1073741824 | bytes 2097152 | tf_op jit(solution)/shard_map/attend_far/pallas_call | solution.py:486
  51.4 0.4 collective-permute-start.2
  51.8 1.1 %attend_near.1.keep_ref = f32[3,256,128]{2,1,0:T(8,128)S(1)} custom-call(bf16[512,128]{1,0:T(8,128)(2,1)S(1)} %get-tuple-element.16.q_ref, f32[12,128]{1,0:T(8,128)S(1)} %get-tuple-element.17.where_ref, f32[128,128]{1,0:T(8,128)S(1)} %get-tuple-element.18.start_ref, bf16[16,120,128]{2,1,0:T(8,128)(2,1)S(1)} %all_to_all.11.mine_ref, ...), custom_call_target="tpu_custom_call" | custom-call | flops 1073741824 | bytes 2097152 | tf_op jit(solution)/shard_map/attend_near/pallas_call | solution.py:488
  52.9 1.7 %collective-permute-done.2.come_ref = bf16[272,128]{1,0:T(8,128)(2,1)S(1)} collective-permute-done((bf16[272,128]{1,0:T(8,128)(2,1)S(1)}, bf16[272,128]{1,0:T(8,128)(2,1)S(1)}, u32[]{:S(2)}, u32[]{:S(2)}) %collective-permute-start.2) | collective-permute-done | bytes 69664 | tf_op jit(solution)/shard_map/ppermute | solution.py:487
  54.6 0.8 %combine.1 = bf16[128,256]{1,0:T(8,128)(2,1)} custom-call(f32[3,256,128]{2,1,0:T(8,128)S(1)} %attend_near.1.keep_ref, bf16[272,128]{1,0:T(8,128)(2,1)S(1)} %collective-permute-done.2.come_ref), custom_call_target="tpu_custom_call" | custom-call | tf_op jit(solution)/shard_map/combine/pallas_call | solution.py:489
Async XLA Ops:
  0.0 48.8 %copy-start = (s32[1,16]{1,0:T(1,128)S(1)}, s32[1,16]{1,0:T(1,128)}, u32[]{:S(2)}) copy-start(s32[1,16]{1,0:T(1,128)} %mask_ref.1) | copy-start | bytes 196
  5.1 13.9 %collective-permute-start = (bf16[512,128]{1,0:T(8,128)(2,1)S(1)}, bf16[512,128]{1,0:T(8,128)(2,1)S(1)}, u32[]{:S(2)}, u32[]{:S(2)}) collective-permute-start(bf16[512,128]{1,0:T(8,128)(2,1)S(1)} %get-tuple-element.13), channel_id=1, source_target_pairs={{0,2},{1,3},{2,0},{3,1},{4,6},{5,7},{6,4},{7,5},{8,10},{9,11},{10,... | collective-permute-start | bytes 393224 | tf_op jit(solution)/shard_map/ppermute | solution.py:468
  46.3 4.0 %collective-permute-start.1 = (bf16[16,120,128]{2,1,0:T(8,128)(2,1)S(1)}, bf16[16,120,128]{2,1,0:T(8,128)(2,1)S(1)}, u32[]{:S(2)}, u32[]{:S(2)}) collective-permute-start(bf16[16,120,128]{2,1,0:T(8,128)(2,1)S(1)} %all_to_all.11.mine_ref), channel_id=1, source_target_pairs={{0,1},{1,0},{2,3},{3,2},{4,5},{5,4},{6,7},{7,6},{8,9},{9,8},{10,11... | collective-permute-start | bytes 1474568 | tf_op jit(solution)/shard_map/ppermute | solution.py:472
  51.4 3.2 %collective-permute-start.2 = (bf16[272,128]{1,0:T(8,128)(2,1)S(1)}, bf16[272,128]{1,0:T(8,128)(2,1)S(1)}, u32[]{:S(2)}, u32[]{:S(2)}) collective-permute-start(bf16[272,128]{1,0:T(8,128)(2,1)S(1)} %attend_far.1), channel_id=1, source_target_pairs={{0,2},{1,3},{2,0},{3,1},{4,6},{5,7},{6,4},{7,5},{8,10},{9,11},{10,... | collective-permute-start | bytes 208904 | tf_op jit(solution)/shard_map/ppermute | solution.py:487

commit v8 on v5

--- a/solution.py
+++ b/solution.py
@@ -322,7 +322,7 @@
             keep_ref[2] = jnp.broadcast_to(total, (count, HD))
             return
         send_ref = rest[0]
-        send_ref[0:count, :] = (mix / jnp.maximum(total, 1.0e-30)).astype(bf16)
+        send_ref[0:count, :] = (mix * (1.0 / jnp.maximum(total, 1.0e-30))).astype(bf16)
         rows = []
         for column in (top, total):
             for e in range(2):

time: 55.6 us -> 55.6 us (level)
  no operation moved by 1% of the time
where the time goes in v8:
time: 55.6 us; the launch traced here: 55.4 us
  blocking collectives  38.8 us (70%)
  Pallas kernels  9.53 us (17%)
  starting transfers between devices  5.13 us (9%)
  waiting for transfers between devices  1.98 us (4%)
    all_to_all x1, blocking collectives, body(): mine = lax.all_to_all(payload, 'seq', 0, 0)  27.1 us
    all_to_all x1, blocking collectives, body(): kv_mine = lax.all_to_all(kv_send, 'head', 0, 0)  11.7 us
    pallas_call x1, Pallas kernels, project_call(): call(*(pltpu.with_memory_space_constraint(array, pltpu.HBM) for array in...  5.11 us
    ppermute x1, starting transfers between devices, body(): other = lax.ppermute(mine, 'head', core_swap)  2.54 us
    ppermute x1, starting transfers between devices, body(): shared = lax.ppermute(share, 'head', chip_swap)  2.21 us
    ppermute x1, waiting for transfers between devices, body(): come = lax.ppermute(send, 'head', chip_swap)  1.75 us
    pallas_call x1, Pallas kernels, body(): pl.pallas_call(place_kernel, name='place', out_shape=(jax.ShapeDtypeStruc...  1.26 us
    pallas_call x1, Pallas kernels, body(): keep = attend_call(False)(merged, where, start, mine, other)  1.12 us
  transfers between devices with their start and end apart: 3, of which 2 were waited for; matrix products, arithmetic and copies ran while one was open for 0% of the time, Pallas kernels for 4%

profile of v8, /device:TPU:1, one launch (start us, length us, event | category | flops | bytes accessed | tf_op | source)
XLA Modules:
  0.0 55.4 jit_solution(1740389542929909015)
XLA Ops:
  0.0 0.0 copy-start
  0.0 5.1 %project.1 = (bf16[16,8,128]{2,1,0:T(8,128)(2,1)S(1)}, bf16[512,128]{1,0:T(8,128)(2,1)S(1)}, f32[432,128]{1,0:T(8,128)S(1)}, f32[384,128]{1,0:T(8,128)S(1)}) custom-call(bf16[128,8192]{1,0:T(8,128)(2,1)} %x_hbm.1, bf16[48,8192]{1,0:T(8,128)(2,1)} %img_hbm.1, bf16[8192,256]{1,0:T(8,128)(2,1)} %wq_hbm.1, bf16[32,8192]{1,0:T(8,128)(2,1)} %bitcast.7, ...), custom_call_target="tpu_custom_call" | custom-call | tf_op jit(solution)/shard_map/project/pallas_call | solution.py:404
  5.1 2.2 %collective-permute-start = (bf16[512,128]{1,0:T(8,128)(2,1)S(1)}, bf16[512,128]{1,0:T(8,128)(2,1)S(1)}, u32[]{:S(2)}, u32[]{:S(2)}) collective-permute-start(bf16[512,128]{1,0:T(8,128)(2,1)S(1)} %get-tuple-element.13), channel_id=1, source_target_pairs={{0,2},{1,3},{2,0},{3,1},{4,6},{5,7},{6,4},{7,5},{8,10},{9,11},{10,... | collective-permute-start | bytes 393224 | tf_op jit(solution)/shard_map/ppermute | solution.py:459
  7.3 11.7 %all_to_all.10.kv_ref = bf16[16,8,128]{2,1,0:T(8,128)(2,1)S(1)} all-to-all(bf16[16,8,128]{2,1,0:T(8,128)(2,1)S(1)} %get-tuple-element.14), channel_id=1, replica_groups=mesh['seq'=16,'head'=16] {'head'}, dimensions={0} | all-to-all | bytes 65536 | tf_op jit(solution)/shard_map/all_to_all | solution.py:460
  19.0 0.0 collective-permute-done.share_ref
  19.0 0.2 panel.1
  19.2 27.1 %all_to_all.11.mine_ref = bf16[16,120,128]{2,1,0:T(8,128)(2,1)S(1)} all-to-all(bf16[16,120,128]{2,1,0:T(8,128)(2,1)S(1)} %panel.1), channel_id=1, replica_groups=mesh['seq'=16,'head'=16] {'seq'}, dimensions={0} | all-to-all | bytes 983040 | tf_op jit(solution)/shard_map/all_to_all | solution.py:462
  46.3 2.5 %collective-permute-start.1 = (bf16[16,120,128]{2,1,0:T(8,128)(2,1)S(1)}, bf16[16,120,128]{2,1,0:T(8,128)(2,1)S(1)}, u32[]{:S(2)}, u32[]{:S(2)}) collective-permute-start(bf16[16,120,128]{2,1,0:T(8,128)(2,1)S(1)} %all_to_all.11.mine_ref), channel_id=1, source_target_pairs={{0,1},{1,0},{2,3},{3,2},{4,5},{5,4},{6,7},{7,6},{8,9},{9,8},{10,11... | collective-permute-start | bytes 1474568 | tf_op jit(solution)/shard_map/ppermute | solution.py:463
  48.8 0.0 copy-done
  48.8 1.3 %place.1 = (bf16[512,128]{1,0:T(8,128)(2,1)S(1)}, f32[12,128]{1,0:T(8,128)S(1)}, f32[128,128]{1,0:T(8,128)S(1)}) custom-call(f32[384,128]{1,0:T(8,128)S(1)} %get-tuple-element.12.own_ref, bf16[512,128]{1,0:T(8,128)(2,1)S(1)} %collective-permute-done.share_ref, bf16[16,120,128]{2,1,0:T(8,128)(2,1)S(1)} %all_to_all.11.mine_ref, s32[1,16]{1,0:T(1,128)S(1)} %copy-done), custom_call_target="tpu_custom_call" | custom-call | flops 268435456 | bytes 1048576 | tf_op jit(solution)/shard_map/place/pallas_call | solution.py:464
  50.1 0.2 collective-permute-done.1.other_ref
  50.3 1.1 %attend_far.1 = bf16[272,128]{1,0:T(8,128)(2,1)S(1)} custom-call(bf16[512,128]{1,0:T(8,128)(2,1)S(1)} %get-tuple-element.16.q_ref, f32[12,128]{1,0:T(8,128)S(1)} %get-tuple-element.17.where_ref, f32[128,128]{1,0:T(8,128)S(1)} %get-tuple-element.18.start_ref, bf16[16,120,128]{2,1,0:T(8,128)(2,1)S(1)} %all_to_all.11.mine_ref, ...), custom_call_target="tpu_custom_call" | custom-call | flops 1073741824 | bytes 2097152 | tf_op jit(solution)/shard_map/attend_far/pallas_call | solution.py:477
  51.4 0.4 collective-permute-start.2
  51.8 1.1 %attend_near.1.keep_ref = f32[3,256,128]{2,1,0:T(8,128)S(1)} custom-call(bf16[512,128]{1,0:T(8,128)(2,1)S(1)} %get-tuple-element.16.q_ref, f32[12,128]{1,0:T(8,128)S(1)} %get-tuple-element.17.where_ref, f32[128,128]{1,0:T(8,128)S(1)} %get-tuple-element.18.start_ref, bf16[16,120,128]{2,1,0:T(8,128)(2,1)S(1)} %all_to_all.11.mine_ref, ...), custom_call_target="tpu_custom_call" | custom-call | flops 1073741824 | bytes 2097152 | tf_op jit(solution)/shard_map/attend_near/pallas_call | solution.py:479
  52.9 1.7 %collective-permute-done.2.come_ref = bf16[272,128]{1,0:T(8,128)(2,1)S(1)} collective-permute-done((bf16[272,128]{1,0:T(8,128)(2,1)S(1)}, bf16[272,128]{1,0:T(8,128)(2,1)S(1)}, u32[]{:S(2)}, u32[]{:S(2)}) %collective-permute-start.2) | collective-permute-done | bytes 69664 | tf_op jit(solution)/shard_map/ppermute | solution.py:478
  54.6 0.8 %combine.1 = bf16[128,256]{1,0:T(8,128)(2,1)} custom-call(f32[3,256,128]{2,1,0:T(8,128)S(1)} %attend_near.1.keep_ref, bf16[272,128]{1,0:T(8,128)(2,1)S(1)} %collective-permute-done.2.come_ref), custom_call_target="tpu_custom_call" | custom-call | tf_op jit(solution)/shard_map/combine/pallas_call | solution.py:480
Async XLA Ops:
  0.0 48.8 %copy-start = (s32[1,16]{1,0:T(1,128)S(1)}, s32[1,16]{1,0:T(1,128)}, u32[]{:S(2)}) copy-start(s32[1,16]{1,0:T(1,128)} %mask_ref.1) | copy-start | bytes 196
  5.1 13.9 %collective-permute-start = (bf16[512,128]{1,0:T(8,128)(2,1)S(1)}, bf16[512,128]{1,0:T(8,128)(2,1)S(1)}, u32[]{:S(2)}, u32[]{:S(2)}) collective-permute-start(bf16[512,128]{1,0:T(8,128)(2,1)S(1)} %get-tuple-element.13), channel_id=1, source_target_pairs={{0,2},{1,3},{2,0},{3,1},{4,6},{5,7},{6,4},{7,5},{8,10},{9,11},{10,... | collective-permute-start | bytes 393224 | tf_op jit(solution)/shard_map/ppermute | solution.py:459
  46.3 4.0 %collective-permute-start.1 = (bf16[16,120,128]{2,1,0:T(8,128)(2,1)S(1)}, bf16[16,120,128]{2,1,0:T(8,128)(2,1)S(1)}, u32[]{:S(2)}, u32[]{:S(2)}) collective-permute-start(bf16[16,120,128]{2,1,0:T(8,128)(2,1)S(1)} %all_to_all.11.mine_ref), channel_id=1, source_target_pairs={{0,1},{1,0},{2,3},{3,2},{4,5},{5,4},{6,7},{7,6},{8,9},{9,8},{10,11... | collective-permute-start | bytes 1474568 | tf_op jit(solution)/shard_map/ppermute | solution.py:463
  51.4 3.2 %collective-permute-start.2 = (bf16[272,128]{1,0:T(8,128)(2,1)S(1)}, bf16[272,128]{1,0:T(8,128)(2,1)S(1)}, u32[]{:S(2)}, u32[]{:S(2)}) collective-permute-start(bf16[272,128]{1,0:T(8,128)(2,1)S(1)} %attend_far.1), channel_id=1, source_target_pairs={{0,2},{1,3},{2,0},{3,1},{4,6},{5,7},{6,4},{7,5},{8,10},{9,11},{10,... | collective-permute-start | bytes 208904 | tf_op jit(solution)/shard_map/ppermute | solution.py:478
